TPU v7x, 512 devices: a whole 4x8x8 slice. The times are simulated.
512 devices in a mesh: leaf: 8 (over z), row: 8 (over y_lo, x), col: 8 (over y_hi, core).
Axes of the slice: x: 4, y: 8 (y_hi: 4, y_lo: 2; y = y_hi * 2 + y_lo), z: 8, core: 2. Of those that a mesh axis runs over, the one named last changes fastest.
Arguments:
- child_update: bfloat16 [8, 3072, 3072], P('leaf', 'row', 'col'), as said below
- block_map: int32 [8, 24], replicated, may hold values from 0 to 63, as said below
- pivot_entries: float32 [8, 4096, 512], P('leaf', 'row'), as said below
- pivot_count: int32 [4], replicated, may hold values from 256 to 512, as said below
Outputs:
- factor: float32 [8, 4096, 512], P('leaf', 'row')
- update: bfloat16 [8, 4096, 8192], P('leaf', 'row', 'col')
Inputs may be any that keep to these rules, and one draw needn't show every extreme that they name: `child_update`: each child's block is symmetric positive definite. `block_map`: each row lists 3072/128 distinct parent blocks in increasing order and includes the first and the last block; rows of odd children list, besides the first block, only blocks from 32 on. `pivot_entries`: the first 512 rows of each even leaf slice form a symmetric positive definite block. `pivot_count`: some parent has exactly 512 pivots.
All inputs are finite; a program needn't handle non-finite values.
Results may differ from a plain program's by a relative error of at most 0.01.
Values may be sent and summed in bfloat16 or wider, within the bound.
A program may use at most 64 MiB of HBM per device.

v0:
```python
import jax
import jax.numpy as jnp
from jax import lax
from jax.sharding import PartitionSpec as P

NF = 8192
BLK = 128
PMAX = 512


def from_partner(shard, axis, apart):
    return lax.ppermute(shard, axis, [(i, i ^ 1 << apart) for i in range(lax.axis_size(axis))])


def spread(value, axis, source):
    kept = jnp.where(lax.axis_index(axis) == source, value, 0).astype(value.dtype)
    return lax.psum(kept, axis)


def source_index(block_list, targets):
    matches = block_list[None, :] == (targets // BLK)[:, None]
    present = jnp.any(matches, axis=1)
    slots = jnp.arange(block_list.shape[0], dtype=jnp.int32)
    position = jnp.sum(jnp.where(matches, slots[None, :], 0), axis=1)
    return jnp.where(present, position * BLK + targets % BLK, -1)


def pick_entries(shard_piece, sources, along):
    extent = shard_piece.shape[along]
    inside = (sources >= 0) & (sources >= 0) & (sources < extent)
    picked = jnp.take(shard_piece, jnp.clip(sources, 0, extent - 1), axis=along).astype(jnp.float32)
    shaped = inside[:, None] if along == 0 else inside[None, :]
    return jnp.where(shaped, picked, 0.0)


def solve_rows(pivot_square, columns, pivot_mask):
    pivot_pair = pivot_mask[:, None] & pivot_mask[None, :]
    square = jnp.where(pivot_pair, pivot_square, jnp.eye(PMAX, dtype=jnp.float32))
    chol_lower = jnp.linalg.cholesky(square)
    return lax.linalg.triangular_solve(
        chol_lower, columns, left_side=False, lower=True, transpose_a=True
    )


def on_device(child_update, block_map, pivot_entries, pivot_count):
    leaf_id = lax.axis_index("leaf")
    half_id = leaf_id % 2
    parent_id = leaf_id // 2
    row_count = lax.axis_size("row")
    col_count = lax.axis_size("col")
    row_id = lax.axis_index("row")
    col_id = lax.axis_index("col")
    child_block = child_update[0]
    own_map = block_map[leaf_id]
    owner_rows = pivot_entries.shape[1]
    range_cols = NF // col_count
    half_rows = NF // 2
    steps_rows = jnp.arange(owner_rows, dtype=jnp.int32)
    row_targets = jnp.concatenate(
        [row_id * owner_rows + steps_rows, half_rows + row_id * owner_rows + steps_rows]
    )
    col_targets = col_id * range_cols + jnp.arange(range_cols, dtype=jnp.int32)
    row_sources = source_index(own_map, row_targets)
    col_sources = source_index(own_map, col_targets)
    strip = pick_entries(lax.all_gather(child_block, "col", axis=1, tiled=True), col_sources, 1)
    both_halves = pick_entries(
        lax.all_gather(strip.astype(jnp.bfloat16), "row", axis=0, tiled=True), row_sources, 0
    )
    both_halves = both_halves.astype(jnp.bfloat16)
    own_half = jnp.where(half_id == 0, both_halves[:owner_rows], both_halves[owner_rows:])
    other_half = jnp.where(half_id == 0, both_halves[owner_rows:], both_halves[:owner_rows])
    from_sibling = from_partner(other_half, "leaf", 0)
    assembled = own_half.astype(jnp.float32) + from_sibling.astype(jnp.float32)
    pivots = pivot_count[parent_id]
    pivot_mask = jnp.arange(PMAX, dtype=jnp.int32) < pivots
    local_columns = jnp.where(pivot_mask[None, :], assembled[:, :PMAX] + pivot_entries[0], 0.0)
    received = (
        from_partner(local_columns.astype(jnp.bfloat16), "leaf", 0).astype(local_columns.dtype),
        from_partner(local_columns.astype(jnp.bfloat16), "leaf", 0).astype(local_columns.dtype),
    )
    square_piece = jnp.where(half_id == 0, local_columns, received[0])
    lower_rows = jnp.where(half_id == 0, local_columns, received[1])
    upper_rows = jnp.where(half_id == 0, received[1], local_columns)
    pair_columns = jnp.concatenate([lower_rows, upper_rows], axis=0)
    pivot_square = spread(square_piece.astype(jnp.bfloat16), "row", 0).astype(square_piece.dtype)
    factor_pair = spread(solve_rows(pivot_square, pair_columns, pivot_mask), "col", 0)
    factor_rows = jnp.where(half_id == 0, factor_pair[:owner_rows], factor_pair[owner_rows:])
    rounded_pair = factor_pair.astype(jnp.bfloat16)
    rounded = jnp.where(half_id == 0, rounded_pair[:owner_rows], rounded_pair[owner_rows:])
    per_range = range_cols // owner_rows
    first_owner = col_id * per_range
    owner_half = first_owner // row_count
    range_source = jnp.where(owner_half == 0, rounded_pair[:owner_rows], rounded_pair[owner_rows:])
    gathered = []
    for part_id in range(per_range):
        gathered.append(spread(range_source, "row", (first_owner + part_id) % row_count))
    far_rows = jnp.concatenate(gathered, axis=0)
    product = lax.dot_general(
        rounded, far_rows, (((1,), (1,)), ((), ())), preferred_element_type=jnp.float32
    )
    schur_part = assembled - product
    row_true = half_id * half_rows + row_id * owner_rows + steps_rows
    keep_rows = row_true >= pivots
    keep_cols = col_targets >= pivots
    update = jnp.where(keep_rows[:, None] & keep_cols[None, :], schur_part, 0.0).astype(
        jnp.bfloat16
    )
    return (factor_rows[None], update[None])


def solution(mesh):
    return jax.shard_map(
        on_device,
        mesh=mesh,
        in_specs=(P("leaf", "row", "col"), P(), P("leaf", "row", None), P()),
        out_specs=(P("leaf", "row", None), P("leaf", "row", "col")),
        check_vma=False,
    )
```

profile of v0, /device:TPU:1, one launch (start us, length us, event | category | flops | bytes accessed | tf_op | source)
XLA Modules:
  0.0 644.8 jit_solution(12378663692728715487)
XLA Ops:
  7.2 1.8 copy.38
  9.6 47.6 %all-gather.6.cloned.1.call-done = bf16[1,384,3072]{1,2,0:T(8,128)(2,1)} async-done(((bf16[1,384,384]{1,2,0:T(8,128)(2,1)}), bf16[1,384,3072]{1,2,0:T(8,128)(2,1)}) %all-gather.6.cloned.1.call-update) | async-done | bytes 2359312 | tf_op jit(solution)/shard_map/all_gather | solution.py:65
  57.1 5.7 gather_fusion
  62.9 1.2 fusion.17
  64.3 75.0 %all-gather.4.cloned.1.call-done = bf16[3072,1024]{0,1:T(8,128)(2,1)} async-done(((bf16[384,1024]{0,1:T(8,128)(2,1)}), bf16[3072,1024]{0,1:T(8,128)(2,1)}) %all-gather.4.cloned.1.call-update) | async-done | bytes 6291472 | tf_op jit(solution)/shard_map/all_gather | solution.py:67
  139.3 8.6 %copy.39 = bf16[3072,1024]{1,0:T(8,128)(2,1)} copy(bf16[3072,1024]{0,1:T(8,128)(2,1)} %all-gather.4.cloned.1.call-done) | data formatting | bytes 12582912 | tf_op jit(solution)/shard_map/all_gather | solution.py:67
  147.9 8.6 %gather_fusion.1 = bf16[1024,1024]{1,0:T(8,128)(2,1)S(1)} fusion(bf16[3072,1024]{1,0:T(8,128)(2,1)} %copy.39, s32[1024]{0:T(1024)S(1)} %broadcast_clamp_fusion), kind=kCustom, calls=%fused_computation.1 | custom fusion | bytes 4198400 | tf_op jit(solution)/shard_map/jit(_take)/gather | solution.py:31
  156.5 2.6 copy.40
  159.0 2.2 select_convert_fusion
  161.3 1.1 broadcast_select_fusion
  162.3 3.3 collective-permute-start
  165.6 1.3 copy.41
  168.1 20.3 %collective-permute-done = bf16[512,1024]{0,1:T(8,128)(2,1)} collective-permute-done((bf16[512,1024]{0,1:T(8,128)(2,1)}, bf16[512,1024]{0,1:T(8,128)(2,1)}, u32[]{:S(2)}, u32[]{:S(2)}) %collective-permute-start) | collective-permute-done | bytes 1048608 | tf_op jit(solution)/shard_map/ppermute | solution.py:12
  188.4 1.7 convert_add_fusion
  190.1 1.3 copy-done.2
  191.7 3.3 collective-permute-start.1
  195.0 10.4 %collective-permute-done.1 = bf16[512,512]{0,1:T(8,128)(2,1)S(1)} collective-permute-done((bf16[512,512]{0,1:T(8,128)(2,1)S(1)}, bf16[512,512]{0,1:T(8,128)(2,1)S(1)}, u32[]{:S(2)}, u32[]{:S(2)}) %collective-permute-start.1) | collective-permute-done | bytes 524320 | tf_op jit(solution)/shard_map/ppermute | solution.py:12
  205.4 1.0 convert_select_fusion.3
  207.0 1.2 convert_select_fusion
  208.2 80.0 %all-reduce.6.cloned.1.call-done = bf16[512,512]{0,1:T(8,128)(2,1)} async-done(((bf16[512,512]{0,1:T(8,128)(2,1)}), bf16[512,512]{0,1:T(8,128)(2,1)}) %all-reduce.6.cloned.1.call-update) | async-done | bytes 524304 | tf_op jit(solution)/shard_map/psum | solution.py:17
  288.2 2.2 convert_select_fusion.2
  290.4 1.6 copy.42
  292.0 1.3 fusion.16
  293.3 1.0 copy-done.5
  294.3 11.7 %cholesky.103 = f32[128,128]{1,0:T(8,128)S(1)} custom-call(f32[128,128]{1,0:T(8,128)S(1)} %cholesky.263), custom_call_target="Cholesky" | custom-call | tf_op jit(solution)/shard_map/jit(cholesky)/cholesky | solution.py:39
  306.1 9.8 %custom-call.30 = f32[1,128,128]{1,2,0:T(8,128)S(1)} custom-call(f32[1,128,128]{2,1,0:T(8,128)S(1)} %get-tuple-element.59), custom_call_target="InvertDiagBlocksLowerTriangular" | custom-call | tf_op jit(solution)/shard_map/jit(cholesky)/cholesky | solution.py:39
  315.9 1.2 fusion.40
  317.1 1.3 convolution_subtract_fusion
  318.4 11.7 %cholesky.215 = f32[128,128]{1,0:T(8,128)S(1)} custom-call(f32[128,128]{1,0:T(8,128)S(1)} %cholesky.267), custom_call_target="Cholesky" | custom-call | tf_op jit(solution)/shard_map/jit(cholesky)/cholesky | solution.py:39
  330.1 0.7 copy.45
  331.0 0.7 copy.43
  331.7 10.6 %custom-call.31 = f32[1,128,128]{1,2,0:T(8,128)} custom-call(f32[1,128,128]{2,1,0:T(8,128)S(1)} %get-tuple-element.57), custom_call_target="InvertDiagBlocksLowerTriangular" | custom-call | tf_op jit(solution)/shard_map/jit(cholesky)/cholesky | solution.py:39
  342.3 1.0 cholesky.222
  343.3 0.8 constant_dynamic-update-slice_fusion.2
  344.1 1.2 convolution_dynamic-update-slice_fusion
  345.3 1.5 convolution_subtract_fusion.1
  346.8 11.7 %cholesky.236 = f32[128,128]{1,0:T(8,128)S(1)} custom-call(f32[128,128]{1,0:T(8,128)S(1)} %cholesky.272), custom_call_target="Cholesky" | custom-call | tf_op jit(solution)/shard_map/jit(cholesky)/cholesky | solution.py:39
  358.7 9.8 %custom-call.32 = f32[1,128,128]{1,2,0:T(8,128)S(1)} custom-call(f32[1,128,128]{2,1,0:T(8,128)S(1)} %get-tuple-element.55), custom_call_target="InvertDiagBlocksLowerTriangular" | custom-call | tf_op jit(solution)/shard_map/jit(cholesky)/cholesky | solution.py:39
  368.8 1.3 convolution_subtract_fusion.2
  370.1 11.9 %cholesky.253 = f32[128,128]{1,0:T(8,128)S(1)} custom-call(f32[128,128]{1,0:T(8,128)S(1)} %convolution_subtract_fusion.2), custom_call_target="Cholesky" | custom-call | tf_op jit(solution)/shard_map/jit(cholesky)/cholesky | solution.py:39
  382.2 0.6 compare_reduce_fusion.4
  382.8 0.6 compare_reduce_fusion.5
  383.4 0.6 compare_reduce_fusion.3
  384.1 0.7 compare_reduce_fusion.2
  387.3 1.1 select_select_fusion
  388.4 14.3 %while.1 = (s32[]{:T(128)}, f32[512,512]{0,1:T(8,128)}, s32[4,2]{0,1:T(2,128)S(1)}, f32[4,128,128]{2,1,0:T(8,128)}, s32[]{:T(128)}) while((s32[]{:T(128)}, f32[512,512]{0,1:T(8,128)}, s32[4,2]{0,1:T(2,128)S(1)}, f32[4,128,128]{2,1,0:T(8,128)}, s32[]{:T(128)}) %tuple.40), condition=%wide.while_cond, body=%wide.while_body.sunk | while | flops 2 | bytes 393829 | solution.py:40
  389.0 2.3 dynamic-slice.7
  392.6 2.3 dynamic-slice.7
  396.2 2.3 dynamic-slice.7
  399.7 2.2 dynamic-slice.7
  402.0 0.6 bitcast_dynamic-update-slice_fusion.2
  402.7 40.1 %custom-call.33 = f32[4,128,128]{1,2,0:T(8,128)S(1)} custom-call(f32[4,128,128]{2,1,0:T(8,128)} %get-tuple-element.9), custom_call_target="InvertDiagBlocksLowerTriangular" | custom-call | tf_op jit(solution)/shard_map/triangular_solve | solution.py:40
  443.4 1.5 fusion.47
  445.5 1.7 fusion.9
  447.8 2.1 fusion
  450.6 1.6 maximum_select_fusion
  452.2 93.7 %all-reduce.8.cloned.1.call-done = f32[1024,512]{0,1:T(8,128)} async-done(((f32[1024,512]{0,1:T(8,128)}), f32[1024,512]{0,1:T(8,128)}) %all-reduce.8.cloned.1.call-update) | async-done | bytes 2097168 | tf_op jit(solution)/shard_map/psum | solution.py:17
  546.0 1.7 convert_element_type.58
  547.7 1.1 broadcast_select_fusion.3
  550.0 1.2 fusion.7
  551.2 2.7 copy.55
  553.9 78.8 %all-reduce.10.cloned.1.call-done = (bf16[512,512]{0,1:T(8,128)(2,1)}, bf16[512,512]{0,1:T(8,128)(2,1)}) async-done(((bf16[512,512]{0,1:T(8,128)(2,1)}, bf16[512,512]{0,1:T(8,128)(2,1)}), (bf16[512,512]{0,1:T(8,128)(2,1)}, bf16[512,512]{0,1:T(8,128)(2,1)})) %all-reduce.10.cloned.1.call-update) | async-done | bytes 1048592 | tf_op jit(solution)/shard_map/psum | solution.py:17
  632.8 3.0 fusion.6
  635.8 2.3 copy.56
  (83 shorter events, 11.6 us)
Async XLA Ops:
  7.2 2.0 copy-start
  7.2 50.0 %all-gather.6.cloned.1.call-start = ((), (), s32[]{:S(2)}) async-start(), calls=%async_computation.3 | async-start | bytes 2654208 | tf_op jit(solution)/shard_map/all_gather | solution.py:65
  9.1 130.2 %all-gather.4.cloned.1.call-start = ((), (), s32[]{:S(2)}) async-start(), calls=%async_computation | async-start | bytes 7077888 | tf_op jit(solution)/shard_map/all_gather | solution.py:67
  64.1 224.1 %all-reduce.6.cloned.1.call-start = ((), (), s32[]{:S(2)}) async-start(), calls=%async_computation.1 | async-start | bytes 1048576 | tf_op jit(solution)/shard_map/psum | solution.py:17
  161.2 4.4 copy-start.7
  161.2 5.7 copy-start.8
  162.3 26.1 %collective-permute-start = (bf16[512,1024]{0,1:T(8,128)(2,1)}, bf16[512,1024]{0,1:T(8,128)(2,1)}, u32[]{:S(2)}, u32[]{:S(2)}) collective-permute-start(bf16[512,1024]{0,1:T(8,128)(2,1)} %broadcast_select_fusion), channel_id=1, source_target_pairs={{0,64},{64,0},{128,192},{192,128},{256,320},{320,256},{384,448},{4... | collective-permute-start | bytes 3145736 | tf_op jit(solution)/shard_map/ppermute | solution.py:12
  168.1 23.4 %copy-start.4 = (f32[1,512,512]{1,2,0:T(8,128)S(1)}, f32[1,512,512]{1,2,0:T(8,128)}, u32[]{:S(2)}) copy-start(f32[1,512,512]{1,2,0:T(8,128)} %copy.41) | copy-start | bytes 3145732
  190.1 1.4 copy-start.2
  191.7 13.7 %collective-permute-start.1 = (bf16[512,512]{0,1:T(8,128)(2,1)S(1)}, bf16[512,512]{0,1:T(8,128)(2,1)S(1)}, u32[]{:S(2)}, u32[]{:S(2)}) collective-permute-start(bf16[512,512]{0,1:T(8,128)(2,1)S(1)} %get-tuple-element.44), channel_id=1, source_target_pairs={{0,64},{64,0},{128,192},{192,128},{256,320},{320,256},{384,448},{4... | collective-permute-start | bytes 1572872 | tf_op jit(solution)/shard_map/ppermute | solution.py:12
  205.4 1.6 copy-start.6
  206.4 339.6 %all-reduce.8.cloned.1.call-start = ((), (), s32[]{:S(2)}) async-start(), calls=%async_computation.2 | async-start | bytes 4194304 | tf_op jit(solution)/shard_map/psum | solution.py:17
  293.3 1.0 copy-start.5
  452.2 180.6 %all-reduce.10.cloned.1.call-start = ((), (), s32[]{:S(2)}) async-start(), calls=%async_computation.4 | async-start | bytes 2097152 | tf_op jit(solution)/shard_map/psum | solution.py:17
  547.7 2.3 copy-start.1
  551.2 81.5 %copy-start.3 = (f32[512,1024]{0,1:T(8,128)S(1)}, f32[512,1024]{0,1:T(8,128)}, u32[]{:S(2)}) copy-start(f32[512,1024]{0,1:T(8,128)} %copy-done.2) | copy-start | bytes 6291460
Sparse Core Ops, SparseCore 0:
  10.7 46.4 all-gather.5
  64.3 74.9 all-gather.3
  206.5 81.6 all-reduce.5
  452.3 93.6 all-reduce.7
  549.0 83.7 all-reduce.9
where the time goes:
time: 655 us; the launch traced here: 645 us
  waiting for transfers between devices  406 us (62%)
  other arithmetic  141 us (22%)
  local copies, waits for them, and re-layouts  56 us (9%)
  matrix products  17.5 us (3%)
  between operations  17.1 us (3%)
  starting transfers between devices  7.21 us (1%)
    psum x3, waiting for transfers between devices, spread(): return lax.psum(kept, axis)  253 us
    another operation x15, other arithmetic, solve_rows(): chol_lower = jnp.linalg.cholesky(square)  79.9 us
    all_gather x1, waiting for transfers between devices, on_device(): lax.all_gather(strip.astype(jnp.bfloat16), 'row', axis=0, tiled=True)  75 us
    all_gather x1, waiting for transfers between devices, on_device(): lax.all_gather(child_block, 'col', axis=1, tiled=True)  47.6 us
    another operation x3, other arithmetic, solve_rows(): lax.linalg.triangular_solve(chol_lower, columns, left_side=False, lower=T...  41.2 us
    ppermute x2, waiting for transfers between devices, from_partner(): lax.ppermute(shard, axis, [(i, i ^ 1 << apart) for i in range(lax.axis_si...  30.7 us
    gather x3, local copies, waits for them, and re-layouts, pick_entries(): jnp.take(shard_piece, jnp.clip(sources, 0, extent - 1), axis=along)  16.9 us
    another operation x20, local copies, waits for them, and re-layouts  14.2 us
  transfers between devices with their start and end apart: 7, of which 7 were waited for; matrix products, arithmetic and copies ran while one was open for 1% of the time, Pallas kernels for 0%

commit v1 on v0

v1 whole, which is shorter than its diff:
```python
import functools
import jax
import jax.numpy as jnp
from jax import lax
from jax.experimental import pallas as pl
from jax.experimental.pallas import tpu as pltpu
from jax.sharding import PartitionSpec as P

NF = 8192
BLK = 128
PMAX = 512
HI = lax.Precision.HIGHEST


def factor_diag(block):
    lane = lax.broadcasted_iota(jnp.int32, (8, 128), 1)
    sub = lax.broadcasted_iota(jnp.int32, (8, 128), 0)
    tiles = [block[8 * r:8 * r + 8, :] for r in range(16)]
    for j in range(128):
        rb, rs = j // 8, j % 8
        at_j = lane == j
        colb = jnp.broadcast_to(tiles[rb][:, j:j + 1], (8, 128))
        row = jnp.where(at_j[:1], 1.0, tiles[rb][rs:rs + 1, :])
        scaled = jnp.broadcast_to(row * (1.0 / colb[rs:rs + 1, :]), (8, 128))
        for r in range(rb, 16):
            col = colb if r == rb else jnp.broadcast_to(tiles[r][:, j:j + 1], (8, 128))
            new = jnp.where(at_j, 0.0, tiles[r]) - col * scaled
            tiles[r] = jnp.where(sub > rs, new, tiles[r]) if r == rb else new
    full = jnp.concatenate(tiles, axis=0)
    rows = lax.broadcasted_iota(jnp.int32, (128, 128), 0)
    cols = lax.broadcasted_iota(jnp.int32, (128, 128), 1)
    diag = jnp.sum(jnp.where(rows == cols, full, 0.0), axis=1, keepdims=True)
    root = lax.rsqrt(diag)
    root = root * (1.5 - 0.5 * (diag * root) * root)
    return jnp.where(cols < rows, full * root, jnp.where(cols == rows, root, 0.0))

def chol_inverse_kernel(s_ref, out_ref, b_ref):
    b_ref[...] = s_ref[...]
    col_blk = lax.broadcasted_iota(jnp.int32, (128, 512), 1) // 128
    row_blk = lax.broadcasted_iota(jnp.int32, (512, 512), 0) // 128
    all_blk = lax.broadcasted_iota(jnp.int32, (512, 512), 1) // 128
    eye = (lax.broadcasted_iota(jnp.int32, (128, 512), 1) % 128 == lax.broadcasted_iota(jnp.int32, (128, 512), 0)).astype(jnp.float32)

    def step(jb, carry):
        at = pl.ds(pl.multiple_of(jb * 128, 128), 128)
        inv = factor_diag(b_ref[at, at])
        panel = jnp.where(col_blk == jb, eye, b_ref[at, :])
        panel = jnp.dot(inv, panel, precision=HI, preferred_element_type=jnp.float32)
        later = jnp.where(col_blk > jb, panel, 0.0)
        change = lax.dot_general(later, panel, (((0,), (0,)), ((), ())), precision=HI, preferred_element_type=jnp.float32)
        kept = jnp.where((row_blk > jb) & (all_blk == jb), 0.0, b_ref[...])
        b_ref[...] = kept - change
        b_ref[at, :] = panel
        return carry
    lax.fori_loop(0, 4, step, 0)
    out_ref[...] = jnp.where(all_blk <= row_blk, b_ref[...], 0.0)


def chol_inverse(square):
    return pl.pallas_call(
        chol_inverse_kernel,
        out_shape=jax.ShapeDtypeStruct((PMAX, PMAX), jnp.float32),
        in_specs=[pl.BlockSpec(memory_space=pltpu.VMEM)],
        out_specs=pl.BlockSpec(memory_space=pltpu.VMEM),
        scratch_shapes=[pltpu.VMEM((PMAX, PMAX), jnp.float32)],
        cost_estimate=pl.CostEstimate(flops=40_000_000_000, bytes_accessed=2_000_000, transcendentals=0),
        name="chol_inverse",
    )(square)


def copy_or_zero(pos_ref, in_ref, out_ref):
    listed = pos_ref[pl.program_id(0)] >= 0
    block = in_ref[...].reshape(out_ref.shape)

    @pl.when(listed)
    def _():
        out_ref[...] = block

    @pl.when(jnp.logical_not(listed))
    def _():
        out_ref[...] = jnp.zeros_like(out_ref)


def pick_cols(pieces, pos):
    count, rows = pos.shape[0], pieces.shape[1]
    per = pieces.shape[2] // BLK
    return pl.pallas_call(
        copy_or_zero,
        grid_spec=pltpu.PrefetchScalarGridSpec(
            num_scalar_prefetch=1,
            grid=(count,),
            in_specs=[
                pl.BlockSpec(
                    (1, rows, BLK),
                    lambda b, p: (jnp.maximum(p[b], 0) // per, 0, jnp.maximum(p[b], 0) % per),
                )
            ],
            out_specs=pl.BlockSpec((rows, BLK), lambda b, p: (0, b)),
        ),
        out_shape=jax.ShapeDtypeStruct((rows, count * BLK), pieces.dtype),
        cost_estimate=pl.CostEstimate(flops=0, bytes_accessed=4 * rows * count * BLK, transcendentals=0),
        name="pick_cols",
    )(pos, pieces)


def pick_rows(strip, pos):
    count, cols = pos.shape[0], strip.shape[1]
    return pl.pallas_call(
        copy_or_zero,
        grid_spec=pltpu.PrefetchScalarGridSpec(
            num_scalar_prefetch=1,
            grid=(count,),
            in_specs=[pl.BlockSpec((BLK, cols), lambda b, p: (jnp.maximum(p[b], 0), 0))],
            out_specs=pl.BlockSpec((BLK, cols), lambda b, p: (b, 0)),
        ),
        out_shape=jax.ShapeDtypeStruct((count * BLK, cols), strip.dtype),
        cost_estimate=pl.CostEstimate(flops=0, bytes_accessed=4 * cols * count * BLK, transcendentals=0),
        name="pick_rows",
    )(pos, strip)


def to_sibling(x, leaves):
    return lax.ppermute(x, "leaf", [(i, i ^ 1) for i in range(leaves)])


def far_entries(entries, half_id, col_half, leaves, rows, cols):
    rounds = []
    for swap in (0, 1):
        pairs = []
        for leaf in range(leaves):
            for row in range(rows):
                for col in range(cols):
                    here = leaf % 2
                    goes = here if row % 2 == swap else 1 - here
                    target = ((leaf - here + goes) * rows + col) * cols + here * (cols // 2) + row // 2
                    pairs.append(((leaf * rows + row) * cols + col, target))
        rounds.append(lax.ppermute(entries, ("leaf", "row", "col"), pairs))
    same = half_id == col_half
    return jnp.concatenate(
        [jnp.where(same, rounds[0], rounds[1]), jnp.where(same, rounds[1], rounds[0])], axis=0
    )


def on_device(child_update, block_map, pivot_entries, pivot_count):
    leaves, rows, cols = lax.axis_size("leaf"), lax.axis_size("row"), lax.axis_size("col")
    leaf_id, row_id, col_id = lax.axis_index("leaf"), lax.axis_index("row"), lax.axis_index("col")
    half_id = leaf_id % 2
    pivots = pivot_count[leaf_id // 2]
    entries = pivot_entries[0]
    own_rows = entries.shape[0]
    range_cols = NF // cols
    per_row, per_col = own_rows // BLK, range_cols // BLK
    half_blocks = NF // BLK // 2

    own_map = block_map[leaf_id]
    slots = jnp.arange(own_map.shape[0], dtype=jnp.int32)
    blocks = jnp.arange(NF // BLK, dtype=jnp.int32)
    position = jnp.sum(
        jnp.where(own_map[None, :] == blocks[:, None], slots[None, :] + 1, 0), axis=1, dtype=jnp.int32
    ) - 1
    at = functools.partial(lax.dynamic_slice_in_dim, position)
    pos_pivot = position[: PMAX // BLK]
    pos_own = at(half_id * half_blocks + row_id * per_row, per_row)
    pos_other = at((1 - half_id) * half_blocks + row_id * per_row, per_row)
    pos_range = at(col_id * per_col, per_col)

    entries16 = entries.astype(jnp.bfloat16)
    top = jnp.where((row_id == 0) & (half_id == 0), entries16, 0)
    x_count = rows // 2
    steps = (
        [(0, x_count)],
        [(0, 1), (x_count, x_count + 1)],
        [(0, x_count - 1), (1, 2), (x_count, rows - 1), (x_count + 1, x_count + 2)],
    )
    for pairs in steps:
        top = top + lax.ppermute(top, "row", pairs)
    far_own = far_entries(entries16, half_id, col_id // (cols // 2), leaves, rows, cols)

    pieces = lax.all_gather(child_update[0], "col", axis=0)
    pivot_strip = pick_cols(pieces, pos_pivot)
    pivot_all = lax.all_gather(pivot_strip, "row", axis=0, tiled=True)
    pieces, pivot_strip = lax.optimization_barrier((pieces, pivot_strip))
    strip = pick_cols(pieces, pos_range)
    strip_all = lax.all_gather(strip, "row", axis=0, tiled=True)

    square16 = (pick_rows(pivot_all, pos_pivot).astype(jnp.float32) + top.astype(jnp.float32)).astype(
        jnp.bfloat16
    )
    square = square16.astype(jnp.float32) + to_sibling(square16, leaves).astype(jnp.float32)
    pivot_mask = jnp.arange(PMAX, dtype=jnp.int32) < pivots
    square = jnp.where(
        pivot_mask[:, None] & pivot_mask[None, :], square, jnp.eye(PMAX, dtype=jnp.float32)
    )
    inverse = chol_inverse(square)
    strip_all, inverse = lax.optimization_barrier((strip_all, inverse))

    picked = pick_rows(pivot_all, jnp.concatenate([pos_range, pos_other]))
    passed = to_sibling(picked, leaves).astype(jnp.float32)
    far_cols = picked[:range_cols].astype(jnp.float32) + passed[:range_cols] + far_own.astype(jnp.float32)
    own_cols = pick_rows(pivot_all, pos_own).astype(jnp.float32) + passed[range_cols:] + entries
    own_cols = jnp.where(pivot_mask[None, :], own_cols, 0.0)
    far_cols = jnp.where(pivot_mask[None, :], far_cols, 0.0)

    other = to_sibling(pick_rows(strip_all, pos_other), leaves)
    assembled = pick_rows(strip_all, pos_own).astype(jnp.float32) + other.astype(jnp.float32)

    last = (((1,), (1,)), ((), ()))
    factor = lax.dot_general(own_cols, inverse, last, precision=HI, preferred_element_type=jnp.float32)
    far = lax.dot_general(far_cols, inverse, last, precision=HI, preferred_element_type=jnp.float32)
    product = lax.dot_general(
        factor.astype(jnp.bfloat16), far.astype(jnp.bfloat16), last, preferred_element_type=jnp.float32
    )
    row_true = (half_id * half_blocks + row_id * per_row) * BLK + jnp.arange(own_rows, dtype=jnp.int32)
    col_true = col_id * range_cols + jnp.arange(range_cols, dtype=jnp.int32)
    keep = (row_true >= pivots)[:, None] & (col_true >= pivots)[None, :]
    update = jnp.where(keep, assembled - product, 0.0).astype(jnp.bfloat16)
    return (factor[None], update[None])


def solution(mesh):
    return jax.shard_map(
        on_device,
        mesh=mesh,
        in_specs=(P("leaf", "row", "col"), P(), P("leaf", "row", None), P()),
        out_specs=(P("leaf", "row", None), P("leaf", "row", "col")),
        check_vma=False,
    )
```

time: 655 us -> 280 us (0.43)
  the two profiles are of different devices: /device:TPU:1 before, /device:TPU:40 now
where the time goes in v1:
time: 280 us; the launch traced here: 278 us
  waiting for transfers between devices  134 us (48%)
  Pallas kernels  78.9 us (28%)
  starting transfers between devices  30.2 us (11%)
  between operations  14.1 us (5%)
  matrix products  10.6 us (4%)
  other arithmetic  8.38 us (3%)
    pallas_call x1, Pallas kernels, chol_inverse(): pl.pallas_call(chol_inverse_kernel, out_shape=jax.ShapeDtypeStruct((PMAX,...  51 us
    ppermute x3, waiting for transfers between devices, on_device(): top = top + lax.ppermute(top, 'row', pairs)  45.2 us
    all_gather x1, waiting for transfers between devices, on_device(): pieces = lax.all_gather(child_update[0], 'col', axis=0)  43.2 us
    all_gather x1, waiting for transfers between devices, on_device(): strip_all = lax.all_gather(strip, 'row', axis=0, tiled=True)  31.8 us
    pallas_call x5, Pallas kernels, pick_rows(): pl.pallas_call(copy_or_zero, grid_spec=pltpu.PrefetchScalarGridSpec(num_s...  19.7 us
    ppermute x3, starting transfers between devices, to_sibling(): return lax.ppermute(x, 'leaf', [(i, i ^ 1) for i in range(leaves)])  13.5 us
    ppermute x2, starting transfers between devices, far_entries(): rounds.append(lax.ppermute(entries, ('leaf', 'row', 'col'), pairs))  12.7 us
    pallas_call x2, Pallas kernels, pick_cols(): pl.pallas_call(copy_or_zero, grid_spec=pltpu.PrefetchScalarGridSpec(num_s...  8.13 us
  transfers between devices with their start and end apart: 11, of which 7 were waited for; matrix products, arithmetic and copies ran while one was open for 6% of the time, Pallas kernels for 27%

profile of v1, /device:TPU:40, one launch (start us, length us, event | category | flops | bytes accessed | tf_op | source)
XLA Modules:
  0.0 278.4 jit_solution(15628137079211248316)
XLA Ops:
  7.2 0.0 copy-start
  7.2 0.0 all-gather.4.cloned.1.call-start
  7.2 0.7 all-gather.4.cloned.1.call-update
  7.9 0.0 all-gather.6.cloned.1.call-start
  8.0 0.0 copy-done
  8.0 0.1 select_reduce_fusion
  8.1 0.7 fusion.31
  8.8 43.2 %all-gather.4.cloned.1.call-done.in_ref = bf16[8,384,384]{2,1,0:T(8,128)(2,1)} async-done(((bf16[1,384,384]{2,1,0:T(8,128)(2,1)}), bf16[8,384,384]{2,1,0:T(8,128)(2,1)}) %all-gather.4.cloned.1.call-update) | async-done | bytes 2359312 | tf_op jit(solution)/shard_map/all_gather | solution.py:179
  52.0 3.0 %pick_cols.2 = bf16[384,512]{1,0:T(8,128)(2,1)} custom-call(s32[4]{0:T(128)} %get-tuple-element.14.pos_ref, bf16[8,384,384]{2,1,0:T(8,128)(2,1)} %all-gather.4.cloned.1.call-done.in_ref), custom_call_target="tpu_custom_call" | custom-call | bytes 786432 | tf_op jit(solution)/shard_map/pick_cols/pallas_call | solution.py:87
  55.0 0.0 all-gather.6.cloned.1.call-update
  55.0 0.0 all-gather.8.cloned.1.call-start
  55.1 0.7 dynamic_slice.18.pos_ref
  55.7 5.1 %pick_cols.3 = bf16[384,1024]{1,0:T(8,128)(2,1)} custom-call(s32[8]{0:T(128)} %dynamic_slice.18.pos_ref, bf16[8,384,384]{2,1,0:T(8,128)(2,1)} %all-gather.4.cloned.1.call-done.in_ref), custom_call_target="tpu_custom_call" | custom-call | bytes 1572864 | tf_op jit(solution)/shard_map/pick_cols/pallas_call | solution.py:87
  60.9 0.0 all-gather.8.cloned.1.call-update
  60.9 0.0 copy-done.1
  60.9 0.1 broadcast_select_fusion.2
  61.0 1.3 collective-permute-start.1
  62.3 19.9 %collective-permute-done.1 = bf16[512,512]{1,0:T(8,128)(2,1)S(1)} collective-permute-done((bf16[512,512]{1,0:T(8,128)(2,1)S(1)}, bf16[512,512]{1,0:T(8,128)(2,1)S(1)}, u32[]{:S(2)}, u32[]{:S(2)}) %collective-permute-start.1) | collective-permute-done | bytes 524320 | tf_op jit(solution)/shard_map/ppermute | solution.py:176
  82.2 0.1 add.98
  82.3 1.3 collective-permute-start.2
  83.7 22.8 %collective-permute-done.2 = bf16[512,512]{1,0:T(8,128)(2,1)S(1)} collective-permute-done((bf16[512,512]{1,0:T(8,128)(2,1)S(1)}, bf16[512,512]{1,0:T(8,128)(2,1)S(1)}, u32[]{:S(2)}, u32[]{:S(2)}) %collective-permute-start.2) | collective-permute-done | bytes 524320 | tf_op jit(solution)/shard_map/ppermute | solution.py:176
  106.5 0.1 add.99
  106.7 0.0 copy-start.10
  106.7 0.0 copy-start.9
  106.7 1.3 collective-permute-start.3
  108.0 7.2 %all-gather.6.cloned.1.call-done.in_ref = bf16[3072,512]{1,0:T(8,128)(2,1)} async-done(((bf16[384,512]{1,0:T(8,128)(2,1)}), bf16[3072,512]{1,0:T(8,128)(2,1)}) %all-gather.6.cloned.1.call-update) | async-done | bytes 3145744 | tf_op jit(solution)/shard_map/all_gather | solution.py:181
  115.2 3.0 %pick_rows.7 = bf16[512,512]{1,0:T(8,128)(2,1)} custom-call(s32[4]{0:T(128)} %get-tuple-element.14.pos_ref, bf16[3072,512]{1,0:T(8,128)(2,1)} %all-gather.6.cloned.1.call-done.in_ref), custom_call_target="tpu_custom_call" | custom-call | bytes 1048576 | tf_op jit(solution)/shard_map/pick_rows/pallas_call | solution.py:108
  118.1 2.5 collective-permute-done.3
  120.6 1.3 add_convert_fusion
  121.9 3.6 %collective-permute-start.4 = (bf16[512,512]{1,0:T(8,128)(2,1)S(1)}, bf16[512,512]{1,0:T(8,128)(2,1)S(1)}, u32[]{:S(2)}, u32[]{:S(2)}) collective-permute-start(bf16[512,512]{1,0:T(8,128)(2,1)S(1)} %add_convert_fusion), channel_id=1, source_target_pairs={{0,64},{64,0},{128,192},{192,128},{256,320},{320,256},{384,448},{4... | collective-permute-start | bytes 1572872 | tf_op jit(solution)/shard_map/ppermute | solution.py:123
  125.5 3.0 %collective-permute-start.6 = (bf16[512,512]{1,0:T(8,128)(2,1)S(1)}, bf16[512,512]{1,0:T(8,128)(2,1)S(1)}, u32[]{:S(2)}, u32[]{:S(2)}) collective-permute-start(bf16[512,512]{1,0:T(8,128)(2,1)S(1)} %get-tuple-element.9), channel_id=1, source_target_pairs={{0,0},{1,8},{2,16},{3,24},{4,32},{5,40},{6,48},{7,56},{8,64},{9,72... | collective-permute-start | bytes 1572872 | tf_op jit(solution)/shard_map/ppermute | solution.py:137
  128.5 9.7 %collective-permute-start.7 = (bf16[512,512]{1,0:T(8,128)(2,1)S(1)}, bf16[512,512]{1,0:T(8,128)(2,1)S(1)}, u32[]{:S(2)}, u32[]{:S(2)}) collective-permute-start(bf16[512,512]{1,0:T(8,128)(2,1)S(1)} %get-tuple-element.9), channel_id=1, source_target_pairs={{0,64},{1,72},{2,80},{3,88},{4,96},{5,104},{6,112},{7,120},{8,0},{... | collective-permute-start | bytes 1572872 | tf_op jit(solution)/shard_map/ppermute | solution.py:137
  138.2 0.7 dynamic_slice.15
  138.9 0.6 iota_compare_fusion.2
  139.5 0.0 copy-done.8
  139.5 0.0 copy-done.9
  139.5 0.6 pad_add_fusion.pos_ref
  140.1 0.6 add_compare_fusion
  140.8 6.9 %pick_rows.6 = bf16[1536,512]{1,0:T(8,128)(2,1)} custom-call(s32[12]{0:T(128)} %pad_add_fusion.pos_ref, bf16[3072,512]{1,0:T(8,128)(2,1)} %all-gather.6.cloned.1.call-done.in_ref), custom_call_target="tpu_custom_call" | custom-call | bytes 3145728 | tf_op jit(solution)/shard_map/pick_rows/pallas_call | solution.py:108
  147.7 3.0 %collective-permute-start = (bf16[1536,512]{1,0:T(8,128)(2,1)}, bf16[1536,512]{1,0:T(8,128)(2,1)}, u32[]{:S(2)}, u32[]{:S(2)}) collective-permute-start(bf16[1536,512]{1,0:T(8,128)(2,1)} %pick_rows.6), channel_id=1, source_target_pairs={{0,64},{64,0},{128,192},{192,128},{256,320},{320,256},{384,448},{4... | collective-permute-start | bytes 4718600 | tf_op jit(solution)/shard_map/ppermute | solution.py:123
  150.7 0.0 collective-permute-done.4
  150.7 1.2 convert_select_fusion.s_ref
  151.9 51.0 %chol_inverse.1 = f32[512,512]{1,0:T(8,128)} custom-call(f32[512,512]{1,0:T(8,128)} %convert_select_fusion.s_ref), custom_call_target="tpu_custom_call" | custom-call | flops 40000000000 | bytes 2000000 | tf_op jit(solution)/shard_map/chol_inverse/pallas_call | solution.py:60
  203.0 31.8 %all-gather.8.cloned.1.call-done.in_ref = bf16[3072,1024]{1,0:T(8,128)(2,1)} async-done(((bf16[384,1024]{1,0:T(8,128)(2,1)}), bf16[3072,1024]{1,0:T(8,128)(2,1)}) %all-gather.8.cloned.1.call-update) | async-done | bytes 6291472 | tf_op jit(solution)/shard_map/all_gather | solution.py:184
  234.8 3.6 %pick_rows.9 = bf16[512,1024]{1,0:T(8,128)(2,1)} custom-call(s32[4]{0:T(128)} %copy-done.8, bf16[3072,1024]{1,0:T(8,128)(2,1)} %all-gather.8.cloned.1.call-done.in_ref), custom_call_target="tpu_custom_call" | custom-call | bytes 2097152 | tf_op jit(solution)/shard_map/pick_rows/pallas_call | solution.py:108
  238.4 6.9 %collective-permute-start.5 = (bf16[512,1024]{1,0:T(8,128)(2,1)}, bf16[512,1024]{1,0:T(8,128)(2,1)}, u32[]{:S(2)}, u32[]{:S(2)}) collective-permute-start(bf16[512,1024]{1,0:T(8,128)(2,1)} %pick_rows.9), channel_id=1, source_target_pairs={{0,64},{64,0},{128,192},{192,128},{256,320},{320,256},{384,448},{4... | collective-permute-start | bytes 3145736 | tf_op jit(solution)/shard_map/ppermute | solution.py:123
  245.3 0.6 add_compare_fusion.1
  246.0 0.0 collective-permute-done.6
  246.0 0.0 collective-permute-done.7
  246.0 1.1 broadcast_select_fusion.1
  247.1 3.0 %pick_rows.5 = bf16[512,512]{1,0:T(8,128)(2,1)} custom-call(s32[4]{0:T(128)} %get-tuple-element.12.pos_ref, bf16[3072,512]{1,0:T(8,128)(2,1)} %all-gather.6.cloned.1.call-done.in_ref), custom_call_target="tpu_custom_call" | custom-call | bytes 1048576 | tf_op jit(solution)/shard_map/pick_rows/pallas_call | solution.py:108
  250.1 0.0 collective-permute-done
  250.1 1.8 convert_element_type.51
  251.9 3.2 %pick_rows.8 = bf16[512,1024]{1,0:T(8,128)(2,1)} custom-call(s32[4]{0:T(128)} %get-tuple-element.12.pos_ref, bf16[3072,1024]{1,0:T(8,128)(2,1)} %all-gather.8.cloned.1.call-done.in_ref), custom_call_target="tpu_custom_call" | custom-call | bytes 2097152 | tf_op jit(solution)/shard_map/pick_rows/pallas_call | solution.py:108
  255.1 3.8 %fusion.13 = f32[512,512]{1,0:T(8,128)S(1)} fusion(f32[512,512]{1,0:T(8,128)} %chol_inverse.1, f32[1536,512]{1,0:T(8,128)S(1)} %convert_element_type.51, f32[1,512,512]{2,1,0:T(8,128)} %param.6, bf16[512,512]{1,0:T(8,128)(2,1)} %pick_rows.5, pred[512]{0:T(512)(128)(4,1)S(1)} %iota_compare_fusion.2), kind=kOutput, calls=%fused_computation.13 | convolution fusion | flops 1611661312 | bytes 4719104 | tf_op jit(solution)/shard_map/dot_general | solution.py:208
  259.0 0.0 copy-start.4
  259.0 0.0 copy-done.2
  259.0 0.0 copy-done.3
  259.0 0.0 copy-done.6
  259.0 0.0 copy-done.7
  259.0 0.0 copy-start.5
  259.1 3.7 %fusion.6 = bf16[1024,512]{1,0:T(8,128)(2,1)S(1)} fusion(f32[512,512]{1,0:T(8,128)S(1)} %copy-done.3, f32[1536,512]{1,0:T(8,128)S(1)} %convert_element_type.51, bf16[1536,512]{1,0:T(8,128)(2,1)S(1)} %copy-done.2, bf16[512,512]{1,0:T(8,128)(2,1)S(1)} %copy-done.7, bf16[512,512]{1,0:T(8,128)(2,1)S(1)} %copy-done.6, pred[512]{0:T(512)(128)(4,1)S(1)} %iota_compare_fusion.2), kind=kOutput, calls=%fused_computation.7 | convolution fusion | flops 3225944064 | bytes 6291968 | tf_op jit(solution)/shard_map/dot_general | solution.py:209
  262.8 6.0 %collective-permute-done.5 = bf16[512,1024]{1,0:T(8,128)(2,1)} collective-permute-done((bf16[512,1024]{1,0:T(8,128)(2,1)}, bf16[512,1024]{1,0:T(8,128)(2,1)}, u32[]{:S(2)}, u32[]{:S(2)}) %collective-permute-start.5) | collective-permute-done | bytes 1048608 | tf_op jit(solution)/shard_map/ppermute | solution.py:123
  268.8 3.1 %fusion.9 = bf16[1,512,1024]{2,1,0:T(8,128)(2,1)} fusion(bf16[512,1024]{1,0:T(8,128)(2,1)} %collective-permute-done.5, bf16[512,1024]{1,0:T(8,128)(2,1)S(1)} %copy-done.5, pred[1024]{0:T(1024)(128)(4,1)S(1)} %add_compare_fusion, pred[512]{0:T(512)(128)(4,1)S(1)} %add_compare_fusion.1, bf16[1024,512]{1,0:T(8,128)(2,1)S(1)} %fusion.6, f32[512,512]{1,0:T(8,128)S(1)} %fusion.13), kind=kOutput, calls=%fused_computation.8 | convolution fusion | flops 540803072 | bytes 5244416 | tf_op jit(solution)/shard_map/dot_general | solution.py:210
  (12 shorter events, 0.0 us)
Async XLA Ops:
  7.2 0.8 copy-start
  7.2 44.8 %all-gather.4.cloned.1.call-start = ((), (), s32[]{:S(2)}) async-start(), calls=%async_computation | async-start | bytes 2654208 | tf_op jit(solution)/shard_map/all_gather | solution.py:179
  7.9 107.3 %all-gather.6.cloned.1.call-start = ((), (), s32[]{:S(2)}) async-start(), calls=%async_computation.1 | async-start | bytes 3538944 | tf_op jit(solution)/shard_map/all_gather | solution.py:181
  8.8 130.7 %copy-start.8 = (s32[4]{0:T(128)}, s32[4]{0:T(128)S(1)}, u32[]{:S(2)}) copy-start(s32[4]{0:T(128)S(1)} %get-tuple-element.13.pos_ref) | copy-start | bytes 52
  55.0 5.9 %copy-start.1 = (f32[1,512,512]{2,1,0:T(8,128)S(1)}, f32[1,512,512]{2,1,0:T(8,128)}, u32[]{:S(2)}) copy-start(f32[1,512,512]{2,1,0:T(8,128)} %param.6) | copy-start | bytes 3145732
  55.0 179.8 %all-gather.8.cloned.1.call-start = ((), (), s32[]{:S(2)}) async-start(), calls=%async_computation.2 | async-start | bytes 7077888 | tf_op jit(solution)/shard_map/all_gather | solution.py:184
  61.0 21.2 %collective-permute-start.1 = (bf16[512,512]{1,0:T(8,128)(2,1)S(1)}, bf16[512,512]{1,0:T(8,128)(2,1)S(1)}, u32[]{:S(2)}, u32[]{:S(2)}) collective-permute-start(bf16[512,512]{1,0:T(8,128)(2,1)S(1)} %get-tuple-element.8), channel_id=1, source_target_pairs={{0,32},{1,33},{2,34},{3,35},{4,36},{5,37},{6,38},{7,39},{64,96},{6... | collective-permute-start | bytes 1572872 | tf_op jit(solution)/shard_map/ppermute | solution.py:176
  82.3 24.2 %collective-permute-start.2 = (bf16[512,512]{1,0:T(8,128)(2,1)S(1)}, bf16[512,512]{1,0:T(8,128)(2,1)S(1)}, u32[]{:S(2)}, u32[]{:S(2)}) collective-permute-start(bf16[512,512]{1,0:T(8,128)(2,1)S(1)} %add.98), channel_id=1, source_target_pairs={{0,8},{32,40},{1,9},{33,41},{2,10},{34,42},{3,11},{35,43},{4,12},{... | collective-permute-start | bytes 1572872 | tf_op jit(solution)/shard_map/ppermute | solution.py:176
  106.7 31.5 %copy-start.10 = (s32[4]{0:T(128)S(1)}, s32[4]{0:T(128)}, u32[]{:S(2)}) copy-start(s32[4]{0:T(128)} %param.7) | copy-start | bytes 52
  106.7 32.8 %copy-start.9 = (s32[8]{0:T(128)S(1)}, s32[8]{0:T(128)}, u32[]{:S(2)}) copy-start(s32[8]{0:T(128)} %dynamic_slice.18.pos_ref) | copy-start | bytes 100
  106.7 13.9 %collective-permute-start.3 = (bf16[512,512]{1,0:T(8,128)(2,1)S(1)}, bf16[512,512]{1,0:T(8,128)(2,1)S(1)}, u32[]{:S(2)}, u32[]{:S(2)}) collective-permute-start(bf16[512,512]{1,0:T(8,128)(2,1)S(1)} %add.99), channel_id=1, source_target_pairs={{0,24},{8,16},{32,56},{40,48},{1,25},{9,17},{33,57},{41,49},{2,26}... | collective-permute-start | bytes 1572872 | tf_op jit(solution)/shard_map/ppermute | solution.py:176
  121.9 28.8 %collective-permute-start.4 = (bf16[512,512]{1,0:T(8,128)(2,1)S(1)}, bf16[512,512]{1,0:T(8,128)(2,1)S(1)}, u32[]{:S(2)}, u32[]{:S(2)}) collective-permute-start(bf16[512,512]{1,0:T(8,128)(2,1)S(1)} %add_convert_fusion), channel_id=1, source_target_pairs={{0,64},{64,0},{128,192},{192,128},{256,320},{320,256},{384,448},{4... | collective-permute-start | bytes 1572872 | tf_op jit(solution)/shard_map/ppermute | solution.py:123
  125.5 120.5 %collective-permute-start.6 = (bf16[512,512]{1,0:T(8,128)(2,1)S(1)}, bf16[512,512]{1,0:T(8,128)(2,1)S(1)}, u32[]{:S(2)}, u32[]{:S(2)}) collective-permute-start(bf16[512,512]{1,0:T(8,128)(2,1)S(1)} %get-tuple-element.9), channel_id=1, source_target_pairs={{0,0},{1,8},{2,16},{3,24},{4,32},{5,40},{6,48},{7,56},{8,64},{9,72... | collective-permute-start | bytes 1572872 | tf_op jit(solution)/shard_map/ppermute | solution.py:137
  128.5 117.5 %collective-permute-start.7 = (bf16[512,512]{1,0:T(8,128)(2,1)S(1)}, bf16[512,512]{1,0:T(8,128)(2,1)S(1)}, u32[]{:S(2)}, u32[]{:S(2)}) collective-permute-start(bf16[512,512]{1,0:T(8,128)(2,1)S(1)} %get-tuple-element.9), channel_id=1, source_target_pairs={{0,64},{1,72},{2,80},{3,88},{4,96},{5,104},{6,112},{7,120},{8,0},{... | collective-permute-start | bytes 1572872 | tf_op jit(solution)/shard_map/ppermute | solution.py:137
  147.7 102.4 %collective-permute-start = (bf16[1536,512]{1,0:T(8,128)(2,1)}, bf16[1536,512]{1,0:T(8,128)(2,1)}, u32[]{:S(2)}, u32[]{:S(2)}) collective-permute-start(bf16[1536,512]{1,0:T(8,128)(2,1)} %pick_rows.6), channel_id=1, source_target_pairs={{0,64},{64,0},{128,192},{192,128},{256,320},{320,256},{384,448},{4... | collective-permute-start | bytes 4718600 | tf_op jit(solution)/shard_map/ppermute | solution.py:123
  238.4 30.3 %collective-permute-start.5 = (bf16[512,1024]{1,0:T(8,128)(2,1)}, bf16[512,1024]{1,0:T(8,128)(2,1)}, u32[]{:S(2)}, u32[]{:S(2)}) collective-permute-start(bf16[512,1024]{1,0:T(8,128)(2,1)} %pick_rows.9), channel_id=1, source_target_pairs={{0,64},{64,0},{128,192},{192,128},{256,320},{320,256},{384,448},{4... | collective-permute-start | bytes 3145736 | tf_op jit(solution)/shard_map/ppermute | solution.py:123
  255.1 3.9 %copy-start.2 = (bf16[1536,512]{1,0:T(8,128)(2,1)S(1)}, bf16[1536,512]{1,0:T(8,128)(2,1)}, u32[]{:S(2)}) copy-start(bf16[1536,512]{1,0:T(8,128)(2,1)} %pick_rows.6) | copy-start | bytes 4718596
  255.1 3.9 %copy-start.3 = (f32[512,512]{1,0:T(8,128)S(1)}, f32[512,512]{1,0:T(8,128)}, u32[]{:S(2)}) copy-start(f32[512,512]{1,0:T(8,128)} %chol_inverse.1) | copy-start | bytes 3145732
  255.1 3.9 %copy-start.6 = (bf16[512,512]{1,0:T(8,128)(2,1)S(1)}, bf16[512,512]{1,0:T(8,128)(2,1)}, u32[]{:S(2)}) copy-start(bf16[512,512]{1,0:T(8,128)(2,1)} %get-tuple-element.10) | copy-start | bytes 1572868
  255.1 3.9 %copy-start.7 = (bf16[512,512]{1,0:T(8,128)(2,1)S(1)}, bf16[512,512]{1,0:T(8,128)(2,1)}, u32[]{:S(2)}) copy-start(bf16[512,512]{1,0:T(8,128)(2,1)} %get-tuple-element.11) | copy-start | bytes 1572868
  259.0 9.8 %copy-start.4 = (f32[512,512]{1,0:T(8,128)}, f32[512,512]{1,0:T(8,128)S(1)}, u32[]{:S(2)}) copy-start(f32[512,512]{1,0:T(8,128)S(1)} %fusion.13) | copy-start | bytes 3145732
  259.0 9.7 %copy-start.5 = (bf16[512,1024]{1,0:T(8,128)(2,1)S(1)}, bf16[512,1024]{1,0:T(8,128)(2,1)}, u32[]{:S(2)}) copy-start(bf16[512,1024]{1,0:T(8,128)(2,1)} %pick_rows.8) | copy-start | bytes 3145732
Sparse Core Ops, SparseCore 0:
  10.1 41.8 all-gather.3
  55.1 60.0 all-gather.5
  117.8 116.8 all-gather.7

commit v2 on v1

v2 whole, which is shorter than its diff:
```python
import functools
import jax
import jax.numpy as jnp
from jax import lax
from jax.experimental import pallas as pl
from jax.experimental.pallas import tpu as pltpu
from jax.sharding import PartitionSpec as P

NF = 8192
BLK = 128
PMAX = 512
HI = lax.Precision.HIGHEST


def factor_diag(block):
    lane = lax.broadcasted_iota(jnp.int32, (8, 128), 1)
    sub = lax.broadcasted_iota(jnp.int32, (8, 128), 0)
    tiles = [block[8 * r:8 * r + 8, :] for r in range(16)]
    for j in range(128):
        rb, rs = j // 8, j % 8
        at_j = lane == j
        colb = jnp.broadcast_to(tiles[rb][:, j:j + 1], (8, 128))
        row = jnp.where(at_j[:1], 1.0, tiles[rb][rs:rs + 1, :])
        scaled = jnp.broadcast_to(row * (1.0 / colb[rs:rs + 1, :]), (8, 128))
        for r in range(rb, 16):
            col = colb if r == rb else jnp.broadcast_to(tiles[r][:, j:j + 1], (8, 128))
            new = jnp.where(at_j, 0.0, tiles[r]) - col * scaled
            tiles[r] = jnp.where(sub > rs, new, tiles[r]) if r == rb else new
    full = jnp.concatenate(tiles, axis=0)
    rows = lax.broadcasted_iota(jnp.int32, (128, 128), 0)
    cols = lax.broadcasted_iota(jnp.int32, (128, 128), 1)
    diag = jnp.sum(jnp.where(rows == cols, full, 0.0), axis=1, keepdims=True)
    root = lax.rsqrt(diag)
    root = root * (1.5 - 0.5 * (diag * root) * root)
    return jnp.where(cols < rows, full * root, jnp.where(cols == rows, root, 0.0))

def chol_steps_kernel(s_ref, b_ref, *, first, end):
    b_ref[...] = s_ref[...]
    col_blk = lax.broadcasted_iota(jnp.int32, (128, 512), 1) // 128
    row_blk = lax.broadcasted_iota(jnp.int32, (512, 512), 0) // 128
    all_blk = lax.broadcasted_iota(jnp.int32, (512, 512), 1) // 128
    eye = (lax.broadcasted_iota(jnp.int32, (128, 512), 1) % 128 == lax.broadcasted_iota(jnp.int32, (128, 512), 0)).astype(jnp.float32)

    def step(jb, carry):
        at = pl.ds(pl.multiple_of(jb * 128, 128), 128)
        inv = factor_diag(b_ref[at, at])
        panel = jnp.where(col_blk == jb, eye, b_ref[at, :])
        panel = jnp.dot(inv, panel, precision=HI, preferred_element_type=jnp.float32)
        later = jnp.where(col_blk > jb, panel, 0.0)
        change = lax.dot_general(later, panel, (((0,), (0,)), ((), ())), precision=HI, preferred_element_type=jnp.float32)
        kept = jnp.where((row_blk > jb) & (all_blk == jb), 0.0, b_ref[...])
        b_ref[...] = kept - change
        b_ref[at, :] = panel
        return carry
    lax.fori_loop(first, end, step, 0)
    if end == PMAX // BLK:
        b_ref[...] = jnp.where(all_blk <= row_blk, b_ref[...], 0.0)


def chol_steps(state, first, end):
    return pl.pallas_call(
        functools.partial(chol_steps_kernel, first=first, end=end),
        out_shape=jax.ShapeDtypeStruct((PMAX, PMAX), jnp.float32),
        in_specs=[pl.BlockSpec(memory_space=pltpu.VMEM)],
        out_specs=pl.BlockSpec(memory_space=pltpu.VMEM),
        cost_estimate=pl.CostEstimate(
            flops=10_000_000_000 * (end - first), bytes_accessed=2_000_000, transcendentals=0
        ),
        name="chol_steps",
    )(state)


def whole(memory_space=pltpu.VMEM):
    return pl.BlockSpec(memory_space=memory_space)


def expand_cols_kernel(pos_ref, x_ref, out_ref):
    per_in = x_ref.shape[2] // BLK
    per_out = out_ref.shape[2] // BLK
    for b in range(pos_ref.shape[0]):
        pos = pos_ref[b]
        held = jnp.maximum(pos, 0)
        lanes = pl.ds(pl.multiple_of(lax.rem(held, per_in) * BLK, BLK), BLK)
        block = x_ref[lax.div(held, per_in), :, lanes].astype(jnp.float32)
        block = jnp.where(pos >= 0, block, 0.0)
        out_ref[b // per_out, :, (b % per_out) * BLK : (b % per_out + 1) * BLK] = block.astype(out_ref.dtype)


def expand_cols(pieces, pos, ranges):
    rows = pieces.shape[1]
    return pl.pallas_call(
        expand_cols_kernel,
        in_specs=[whole(pltpu.SMEM), whole()],
        out_specs=whole(),
        out_shape=jax.ShapeDtypeStruct((ranges, rows, NF // ranges), pieces.dtype),
        cost_estimate=pl.CostEstimate(flops=0, bytes_accessed=4 * rows * NF, transcendentals=0),
        name="expand_cols",
    )(pos, pieces)


def read_slice(pos, x_ref, per, size):
    held = jnp.maximum(pos, 0)
    rows = pl.ds(pl.multiple_of(lax.rem(held, per) * size, size), size)
    return jnp.where(pos >= 0, x_ref[lax.div(held, per), rows, :].astype(jnp.float32), 0.0)


def expand_pivot_kernel(half_ref, pos_ref, x_ref, out_ref, *, per, per_row, size):
    half = half_ref[0]
    count = pos_ref.shape[0] // 2

    def step(i, carry):
        own, other = half * count + i, (1 - half) * count + i
        entries = pl.ds(pl.multiple_of((per + lax.rem(i, per_row)) * size, size), size)
        entry = x_ref[lax.div(i, per_row), entries, :].astype(jnp.float32)
        mine = read_slice(pos_ref[own], x_ref, per, size) + entry
        out_ref[pl.ds(pl.multiple_of(own * size, size), size), :] = mine.astype(out_ref.dtype)
        theirs = read_slice(pos_ref[other], x_ref, per, size)
        out_ref[pl.ds(pl.multiple_of(other * size, size), size), :] = theirs.astype(out_ref.dtype)
        return carry

    lax.fori_loop(0, count, step, 0)


def expand_pivot(gathered, half_id, pos, per, per_row, size):
    cols = gathered.shape[2]
    return pl.pallas_call(
        functools.partial(expand_pivot_kernel, per=per, per_row=per_row, size=size),
        in_specs=[whole(pltpu.SMEM), whole(pltpu.SMEM), whole()],
        out_specs=whole(),
        out_shape=jax.ShapeDtypeStruct((pos.shape[0] * size, cols), gathered.dtype),
        cost_estimate=pl.CostEstimate(flops=0, bytes_accessed=4_000_000, transcendentals=0),
        name="expand_pivot",
    )(half_id[None], pos, gathered)


def expand_rows_kernel(half_ref, pos_ref, x_ref, own_ref, other_ref, *, per, size):
    half = half_ref[0]
    count = pos_ref.shape[0] // 2

    def step(i, carry):
        at = pl.ds(pl.multiple_of(i * size, size), size)
        mine = read_slice(pos_ref[half * count + i], x_ref, per, size)
        own_ref[at, :] = mine.astype(own_ref.dtype)
        theirs = read_slice(pos_ref[(1 - half) * count + i], x_ref, per, size)
        other_ref[at, :] = theirs.astype(other_ref.dtype)
        return carry

    lax.fori_loop(0, count, step, 0)


def expand_rows(gathered, half_id, pos, per, size):
    shape = jax.ShapeDtypeStruct((pos.shape[0] // 2 * size, gathered.shape[2]), gathered.dtype)
    return pl.pallas_call(
        functools.partial(expand_rows_kernel, per=per, size=size),
        in_specs=[whole(pltpu.SMEM), whole(pltpu.SMEM), whole()],
        out_specs=(whole(), whole()),
        out_shape=(shape, shape),
        cost_estimate=pl.CostEstimate(flops=0, bytes_accessed=6_000_000, transcendentals=0),
        name="expand_rows",
    )(half_id[None], pos, gathered)


def to_sibling(x, leaves):
    return lax.ppermute(x, "leaf", [(i, i ^ 1) for i in range(leaves)])


def add16(a, b):
    return (a.astype(jnp.float32) + b.astype(jnp.float32)).astype(jnp.bfloat16)


def swap_slices(x, blocks, size):
    parts, cols = x.shape[0], x.shape[-1]
    x = x.reshape(parts, blocks, size, cols)
    return jnp.swapaxes(x, 0, 1).reshape(parts * blocks * size, cols)


def swap_axis(x, axis):
    return lax.all_to_all(x, axis, 0, 0, tiled=True)


def on_device(child_update, block_map, pivot_entries, pivot_count):
    leaves, rows, cols = lax.axis_size("leaf"), lax.axis_size("row"), lax.axis_size("col")
    leaf_id, row_id, col_id = lax.axis_index("leaf"), lax.axis_index("row"), lax.axis_index("col")
    half_id = leaf_id % 2
    pivots = pivot_count[leaf_id // 2]
    entries = pivot_entries[0]
    own_rows = entries.shape[0]
    range_cols = NF // cols
    per_row, per_col = own_rows // BLK, range_cols // BLK
    half_blocks = NF // BLK // 2
    size = BLK // cols
    child = child_update[0]
    per = child.shape[0] // BLK

    own_map = block_map[leaf_id]
    slots = jnp.arange(own_map.shape[0], dtype=jnp.int32)
    blocks = jnp.arange(NF // BLK, dtype=jnp.int32)
    position = jnp.sum(
        jnp.where(own_map[None, :] == blocks[:, None], slots[None, :] + 1, 0), axis=1, dtype=jnp.int32
    ) - 1

    slices = jnp.swapaxes(child.reshape(per, cols, size, child.shape[1]), 0, 1)
    pieces = swap_axis(slices.reshape(cols, per * size, child.shape[1]), "col")
    spread_cols = expand_cols(pieces, position, cols)

    entry_slice = lax.dynamic_index_in_dim(
        entries.astype(jnp.bfloat16).reshape(per_row, cols, size, PMAX), col_id, 1, keepdims=False
    ).reshape(per_row * size, PMAX)
    pivot_slice = jnp.concatenate([spread_cols[0, :, :PMAX], entry_slice], axis=0)
    gathered = lax.all_gather(pivot_slice, "row", axis=0)
    spread_cols, pivot_slice = lax.optimization_barrier((spread_cols, pivot_slice))
    strip = swap_axis(spread_cols, "col")

    pivot_own = expand_pivot(gathered, half_id, position, per, per_row, size)
    top = pivot_own[: PMAX // BLK * size]
    top = add16(top, to_sibling(top, leaves))
    top_all = lax.all_gather(top, "col", axis=0)

    pivot_own, strip, top = lax.optimization_barrier((pivot_own, strip, top))
    strip = swap_axis(strip, "row")
    pivot_passed = to_sibling(pivot_own, leaves)

    pivot_mask = jnp.arange(PMAX, dtype=jnp.int32) < pivots
    square = swap_slices(top_all, PMAX // BLK, size).astype(jnp.float32)
    square = jnp.where(
        pivot_mask[:, None] & pivot_mask[None, :], square, jnp.eye(PMAX, dtype=jnp.float32)
    )
    state = chol_steps(square, 0, 2)

    strip, pivot_passed, state = lax.optimization_barrier((strip, pivot_passed, state))
    main_own, main_other = expand_rows(strip, half_id, position, per, size)

    pivot_cols = add16(pivot_own, pivot_passed)
    own_slice = lax.dynamic_slice_in_dim(
        pivot_cols, (half_id * half_blocks + row_id * per_row) * size, per_row * size
    )
    far_slices = pivot_cols.reshape(cols, per_col * size, PMAX)
    own_slices = jnp.broadcast_to(own_slice[None], (cols,) + own_slice.shape)
    sent = jnp.concatenate([far_slices, own_slices], axis=1)
    main_other, sent, state = lax.optimization_barrier((main_other, sent, state))
    main_passed = to_sibling(main_other, leaves)
    moved = swap_axis(sent, "col")
    inverse = chol_steps(state, 2, 4)
    main_passed, moved, inverse = lax.optimization_barrier((main_passed, moved, inverse))
    far_cols = swap_slices(moved[:, : per_col * size], per_col, size).astype(jnp.float32)
    own_cols = swap_slices(moved[:, per_col * size :], per_row, size).astype(jnp.float32)
    own_cols = jnp.where(pivot_mask[None, :], own_cols, 0.0)
    far_cols = jnp.where(pivot_mask[None, :], far_cols, 0.0)

    main = add16(main_own, main_passed).reshape(rows, per_row * size, range_cols)
    assembled = swap_slices(swap_axis(main, "row"), per_row, size).astype(jnp.float32)

    last = (((1,), (1,)), ((), ()))
    factor = lax.dot_general(own_cols, inverse, last, precision=HI, preferred_element_type=jnp.float32)
    far = lax.dot_general(far_cols, inverse, last, precision=HI, preferred_element_type=jnp.float32)
    product = lax.dot_general(
        factor.astype(jnp.bfloat16), far.astype(jnp.bfloat16), last, preferred_element_type=jnp.float32
    )
    row_true = (half_id * half_blocks + row_id * per_row) * BLK + jnp.arange(own_rows, dtype=jnp.int32)
    col_true = col_id * range_cols + jnp.arange(range_cols, dtype=jnp.int32)
    keep = (row_true >= pivots)[:, None] & (col_true >= pivots)[None, :]
    update = jnp.where(keep, assembled - product, 0.0).astype(jnp.bfloat16)
    return (factor[None], update[None])


def solution(mesh):
    return jax.shard_map(
        on_device,
        mesh=mesh,
        in_specs=(P("leaf", "row", "col"), P(), P("leaf", "row", None), P()),
        out_specs=(P("leaf", "row", None), P("leaf", "row", "col")),
        check_vma=False,
    )
```

time: 280 us -> 222 us (0.79)
  the two profiles are of different devices: /device:TPU:40 before, /device:TPU:1 now
where the time goes in v2:
time: 222 us; the launch traced here: 221 us
  blocking collectives  64.3 us (29%)
  Pallas kernels  62 us (28%)
  starting transfers between devices  48.9 us (22%)
  waiting for transfers between devices  14.9 us (7%)
  other arithmetic  12.6 us (6%)
  local copies, waits for them, and re-layouts  9.33 us (4%)
  matrix products  8.06 us (4%)
    pallas_call x2, Pallas kernels, chol_steps(): pl.pallas_call(functools.partial(chol_steps_kernel, first=first, end=end)...  53.3 us
    all_gather x1, blocking collectives, on_device(): gathered = lax.all_gather(pivot_slice, 'row', axis=0)  40.9 us
    all_to_all x5, starting transfers between devices, swap_axis(): return lax.all_to_all(x, axis, 0, 0, tiled=True)  39 us
    all_gather x1, blocking collectives, on_device(): top_all = lax.all_gather(top, 'col', axis=0)  23.3 us
    all_to_all x5, waiting for transfers between devices, swap_axis(): return lax.all_to_all(x, axis, 0, 0, tiled=True)  13.9 us
    ppermute x3, starting transfers between devices, to_sibling(): return lax.ppermute(x, 'leaf', [(i, i ^ 1) for i in range(leaves)])  9.85 us
    convert_element_type x3, other arithmetic, add16(): return (a.astype(jnp.float32) + b.astype(jnp.float32)).astype(jnp.bfloat16)  5.85 us
    dot_general x1, matrix products, on_device(): lax.dot_general(far_cols, inverse, last, precision=HI, preferred_element_...  4.44 us
  transfers between devices with their start and end apart: 8, of which 4 were waited for; matrix products, arithmetic and copies ran while one was open for 7% of the time, Pallas kernels for 26%

profile of v2, /device:TPU:1, one launch (start us, length us, event | category | flops | bytes accessed | tf_op | source)
XLA Modules:
  0.0 220.9 jit_solution(7147846147195730002)
XLA Ops:
  0.6 0.0 copy-start
  0.6 1.7 copy.14
  2.4 10.2 %all-to-all-start = ((bf16[8,48,384]{2,1,0:T(8,128)(2,1)}), bf16[8,48,384]{2,1,0:T(8,128)(2,1)S(1)}, u32[]{:S(2)}, u32[]{:S(2)}) async-start(bf16[8,48,384]{2,1,0:T(8,128)(2,1)} %bitcast.5), calls=%async_computation | async-start | bytes 589824 | tf_op jit(solution)/shard_map/all_to_all | solution.py:178
  12.5 1.3 convert_element_type.94
  13.8 0.0 copy-done
  13.9 0.1 select_reduce_fusion
  14.0 0.5 broadcast_add_fusion.pos_ref
  14.5 9.2 %all-to-all-done.x_ref = bf16[8,48,384]{2,1,0:T(8,128)(2,1)S(1)} async-done(((bf16[8,48,384]{2,1,0:T(8,128)(2,1)}), bf16[8,48,384]{2,1,0:T(8,128)(2,1)S(1)}, u32[]{:S(2)}, u32[]{:S(2)}) %all-to-all-start) | async-done | bytes 294944 | tf_op jit(solution)/shard_map/all_to_all | solution.py:178
  23.7 0.7 copy-done.7
  24.4 2.3 %expand_cols.1 = bf16[8,48,1024]{2,1,0:T(8,128)(2,1)} custom-call(s32[64]{0:T(128)} %broadcast_add_fusion.pos_ref, bf16[8,48,384]{2,1,0:T(8,128)(2,1)} %copy-done.7), custom_call_target="tpu_custom_call" | custom-call | bytes 1572864 | tf_op jit(solution)/shard_map/expand_cols/pallas_call | solution.py:91
  26.7 0.8 slice_bitcast_fusion
  27.5 4.8 %all-to-all-start.1 = ((bf16[8,48,1024]{2,1,0:T(8,128)(2,1)}), bf16[8,48,1024]{2,1,0:T(8,128)(2,1)}, u32[]{:S(2)}, u32[]{:S(2)}) async-start(bf16[8,48,1024]{2,1,0:T(8,128)(2,1)} %expand_cols.1), calls=%async_computation.1 | async-start | bytes 1572864 | tf_op jit(solution)/shard_map/all_to_all | solution.py:178
  32.3 0.0 copy-done.10
  32.3 0.6 dynamic_slice.13
  33.0 40.9 %all-gather = bf16[896,512]{1,0:T(8,128)(2,1)} all-gather(bf16[112,512]{1,0:T(8,128)(2,1)S(1)} %pad_maximum_fusion.1), channel_id=2, replica_groups=mesh['leaf'=8,'row'=8,'col'=8] {'row'}, dimensions={0}, use_global_device_ids=true | all-gather | bytes 1032192 | tf_op jit(solution)/shard_map/all_gather | solution.py:210
  73.9 3.1 %expand_pivot.1 = bf16[1024,512]{1,0:T(8,128)(2,1)} custom-call(s32[1]{0:T(128)} %bitcast.1.half_ref, s32[64]{0:T(128)} %broadcast_add_fusion.pos_ref, bf16[8,112,512]{2,1,0:T(8,128)(2,1)} %bitcast.58), custom_call_target="tpu_custom_call" | custom-call | bytes 4000000 | tf_op jit(solution)/shard_map/expand_pivot/pallas_call | solution.py:126
  77.0 0.8 slice.17
  77.8 4.0 %collective-permute-start = (bf16[64,512]{1,0:T(8,128)(2,1)S(1)}, bf16[64,512]{1,0:T(8,128)(2,1)S(1)}, u32[]{:S(2)}, u32[]{:S(2)}) collective-permute-start(bf16[64,512]{1,0:T(8,128)(2,1)S(1)} %slice.17), channel_id=1, source_target_pairs={{0,64},{64,0},{128,192},{192,128},{256,320},{320,256},{384,448},{4... | collective-permute-start | bytes 196616 | tf_op jit(solution)/shard_map/ppermute | solution.py:164
  81.8 0.6 iota_compare_fusion.2
  82.5 1.0 collective-permute-done
  83.5 0.9 add_convert_fusion.2
  84.3 23.3 %all-gather.1 = bf16[512,512]{1,0:T(8,128)(2,1)S(1)} all-gather(bf16[64,512]{1,0:T(8,128)(2,1)S(1)} %add_convert_fusion.2), channel_id=3, replica_groups=mesh['leaf'=8,'row'=8,'col'=8] {'col'}, dimensions={0}, use_global_device_ids=true | all-gather | bytes 589824 | tf_op jit(solution)/shard_map/all_gather | solution.py:217
  107.7 0.1 copy.15
  107.8 0.0 copy-start.2
  107.8 1.2 bitcast_select_fusion.1.s_ref
  109.0 0.0 all-to-all-done.1
  109.0 3.5 %all-to-all-start.2 = ((bf16[8,48,1024]{2,1,0:T(8,128)(2,1)}), bf16[8,48,1024]{2,1,0:T(8,128)(2,1)S(1)}, u32[]{:S(2)}, u32[]{:S(2)}) async-start(bf16[8,48,1024]{2,1,0:T(8,128)(2,1)} %all-to-all-done.1), calls=%async_computation.2 | async-start | bytes 1572864 | tf_op jit(solution)/shard_map/all_to_all | solution.py:178
  112.5 0.0 copy-done.2
  112.5 3.6 %collective-permute-start.1 = (bf16[1024,512]{1,0:T(8,128)(2,1)S(1)}, bf16[1024,512]{1,0:T(8,128)(2,1)S(1)}, u32[]{:S(2)}, u32[]{:S(2)}) collective-permute-start(bf16[1024,512]{1,0:T(8,128)(2,1)S(1)} %copy-done.2), channel_id=1, source_target_pairs={{0,64},{64,0},{128,192},{192,128},{256,320},{320,256},{384,448},{4... | collective-permute-start | bytes 3145736 | tf_op jit(solution)/shard_map/ppermute | solution.py:164
  116.2 26.6 %chol_steps.2.s_ref = f32[512,512]{1,0:T(8,128)} custom-call(f32[512,512]{1,0:T(8,128)} %bitcast_select_fusion.1.s_ref), custom_call_target="tpu_custom_call" | custom-call | flops 20000000000 | bytes 2000000 | tf_op jit(solution)/shard_map/chol_steps/pallas_call | solution.py:61
  142.8 0.0 collective-permute-done.1
  142.8 1.0 copy-done.9
  143.8 0.0 all-to-all-done.2.x_ref
  143.8 1.8 add_convert_fusion.1
  145.6 0.0 copy-done.6
  145.6 3.3 %expand_rows.1 = (bf16[512,1024]{1,0:T(8,128)(2,1)}, bf16[512,1024]{1,0:T(8,128)(2,1)}) custom-call(s32[1]{0:T(128)} %bitcast.1.half_ref, s32[64]{0:T(128)} %broadcast_add_fusion.pos_ref, bf16[8,48,1024]{2,1,0:T(8,128)(2,1)} %copy-done.6), custom_call_target="tpu_custom_call" | custom-call | bytes 6000000 | tf_op jit(solution)/shard_map/expand_rows/pallas_call | solution.py:153
  149.0 1.3 pad_maximum_fusion
  150.2 5.0 %all-to-all-start.3 = ((bf16[8,192,512]{2,1,0:T(8,128)(2,1)}), bf16[8,192,512]{2,1,0:T(8,128)(2,1)S(1)}, u32[]{:S(2)}, u32[]{:S(2)}) async-start(bf16[8,192,512]{2,1,0:T(8,128)(2,1)} %pad_maximum_fusion), calls=%async_computation.3 | async-start | bytes 3145728 | tf_op jit(solution)/shard_map/all_to_all | solution.py:178
  155.3 2.2 %collective-permute-start.2 = (bf16[512,1024]{1,0:T(8,128)(2,1)}, bf16[512,1024]{1,0:T(8,128)(2,1)}, u32[]{:S(2)}, u32[]{:S(2)}) collective-permute-start(bf16[512,1024]{1,0:T(8,128)(2,1)} %get-tuple-element.23), channel_id=1, source_target_pairs={{0,64},{64,0},{128,192},{192,128},{256,320},{320,256},{384,448},{4... | collective-permute-start | bytes 3145736 | tf_op jit(solution)/shard_map/ppermute | solution.py:164
  157.5 26.7 %chol_steps.3 = f32[512,512]{1,0:T(8,128)} custom-call(f32[512,512]{1,0:T(8,128)} %chol_steps.2.s_ref), custom_call_target="tpu_custom_call" | custom-call | flops 20000000000 | bytes 2000000 | tf_op jit(solution)/shard_map/chol_steps/pallas_call | solution.py:61
  184.2 0.0 collective-permute-done.2
  184.2 0.1 all-to-all-done.3
  184.3 0.0 copy-done.8
  184.3 3.2 %add_convert_fusion = bf16[512,1024]{1,0:T(8,128)(2,1)} fusion(bf16[512,1024]{1,0:T(8,128)(2,1)} %collective-permute-done.2, bf16[512,1024]{1,0:T(8,128)(2,1)S(1)} %copy-done.8), kind=kLoop, calls=%fused_computation.4 | loop fusion | flops 2097152 | bytes 3145728 | tf_op jit(solution)/shard_map/convert_element_type | solution.py:168
  187.5 15.5 %all-to-all-start.4 = ((bf16[8,64,1024]{2,1,0:T(8,128)(2,1)}), bf16[8,64,1024]{2,1,0:T(8,128)(2,1)S(1)}, u32[]{:S(2)}, u32[]{:S(2)}) async-start(bf16[8,64,1024]{2,1,0:T(8,128)(2,1)} %bitcast.56), calls=%async_computation.4 | async-start | bytes 2097152 | tf_op jit(solution)/shard_map/all_to_all | solution.py:178
  203.0 0.6 add_compare_fusion.1
  203.6 0.6 add_compare_fusion
  204.3 0.0 copy-done.1
  204.3 0.0 slice-start
  204.3 0.1 convert_bitcast_fusion
  204.5 0.1 copy.16
  204.6 1.0 slice-done
  205.6 0.3 copy.18
  205.8 0.1 bitcast_select_fusion.2
  206.0 0.8 copy-done.3
  206.8 1.9 fusion.5
  208.6 0.0 copy-start.4
  208.7 0.2 bitcast_select_fusion
  208.9 4.4 %convolution_convert_fusion = bf16[1024,512]{1,0:T(8,128)(2,1)} fusion(f32[1024,512]{1,0:T(8,128)S(1)} %bitcast_select_fusion, f32[512,512]{1,0:T(8,128)S(1)} %copy-done.3), kind=kOutput, calls=%fused_computation.7 | convolution fusion | flops 3221749760 | bytes 4194304 | tf_op jit(solution)/shard_map/dot_general | solution.py:255
  213.4 4.6 %all-to-all-done.4 = bf16[8,64,1024]{2,1,0:T(8,128)(2,1)S(1)} async-done(((bf16[8,64,1024]{2,1,0:T(8,128)(2,1)}), bf16[8,64,1024]{2,1,0:T(8,128)(2,1)S(1)}, u32[]{:S(2)}, u32[]{:S(2)}) %all-to-all-start.4) | async-done | bytes 1048608 | tf_op jit(solution)/shard_map/all_to_all | solution.py:178
  218.0 0.2 copy.17
  218.2 0.0 copy-done.4
  218.2 1.0 copy-done.5
  219.2 1.8 fusion.2
  (15 shorter events, 0.1 us)
Async XLA Ops:
  0.6 13.2 %copy-start = (s32[8,24]{1,0:T(8,128)S(1)}, s32[8,24]{1,0:T(8,128)}, u32[]{:S(2)}) copy-start(s32[8,24]{1,0:T(8,128)} %param.5) | copy-start | bytes 2308
  2.4 21.3 %all-to-all-start = ((bf16[8,48,384]{2,1,0:T(8,128)(2,1)}), bf16[8,48,384]{2,1,0:T(8,128)(2,1)S(1)}, u32[]{:S(2)}, u32[]{:S(2)}) async-start(bf16[8,48,384]{2,1,0:T(8,128)(2,1)} %bitcast.5), calls=%async_computation | async-start | bytes 589824 | tf_op jit(solution)/shard_map/all_to_all | solution.py:178
  12.5 19.8 %copy-start.10 = (s32[4]{0:T(128)S(1)}, s32[4]{0:T(128)}, u32[]{:S(2)}) copy-start(s32[4]{0:T(128)} %param.7) | copy-start | bytes 52
  23.7 0.7 copy-start.7
  27.5 81.5 %all-to-all-start.1 = ((bf16[8,48,1024]{2,1,0:T(8,128)(2,1)}), bf16[8,48,1024]{2,1,0:T(8,128)(2,1)}, u32[]{:S(2)}, u32[]{:S(2)}) async-start(bf16[8,48,1024]{2,1,0:T(8,128)(2,1)} %expand_cols.1), calls=%async_computation.1 | async-start | bytes 1572864 | tf_op jit(solution)/shard_map/all_to_all | solution.py:178
  77.8 5.6 %collective-permute-start = (bf16[64,512]{1,0:T(8,128)(2,1)S(1)}, bf16[64,512]{1,0:T(8,128)(2,1)S(1)}, u32[]{:S(2)}, u32[]{:S(2)}) collective-permute-start(bf16[64,512]{1,0:T(8,128)(2,1)S(1)} %slice.17), channel_id=1, source_target_pairs={{0,64},{64,0},{128,192},{192,128},{256,320},{320,256},{384,448},{4... | collective-permute-start | bytes 196616 | tf_op jit(solution)/shard_map/ppermute | solution.py:164
  107.8 4.7 %copy-start.2 = (bf16[1024,512]{1,0:T(8,128)(2,1)S(1)}, bf16[1024,512]{1,0:T(8,128)(2,1)}, u32[]{:S(2)}) copy-start(bf16[1024,512]{1,0:T(8,128)(2,1)} %expand_pivot.1) | copy-start | bytes 3145732
  109.0 34.8 %all-to-all-start.2 = ((bf16[8,48,1024]{2,1,0:T(8,128)(2,1)}), bf16[8,48,1024]{2,1,0:T(8,128)(2,1)S(1)}, u32[]{:S(2)}, u32[]{:S(2)}) async-start(bf16[8,48,1024]{2,1,0:T(8,128)(2,1)} %all-to-all-done.1), calls=%async_computation.2 | async-start | bytes 1572864 | tf_op jit(solution)/shard_map/all_to_all | solution.py:178
  112.5 30.3 %collective-permute-start.1 = (bf16[1024,512]{1,0:T(8,128)(2,1)S(1)}, bf16[1024,512]{1,0:T(8,128)(2,1)S(1)}, u32[]{:S(2)}, u32[]{:S(2)}) collective-permute-start(bf16[1024,512]{1,0:T(8,128)(2,1)S(1)} %copy-done.2), channel_id=1, source_target_pairs={{0,64},{64,0},{128,192},{192,128},{256,320},{320,256},{384,448},{4... | collective-permute-start | bytes 3145736 | tf_op jit(solution)/shard_map/ppermute | solution.py:164
  142.8 1.0 copy-start.9
  143.8 1.8 copy-start.6
  150.2 34.0 %all-to-all-start.3 = ((bf16[8,192,512]{2,1,0:T(8,128)(2,1)}), bf16[8,192,512]{2,1,0:T(8,128)(2,1)S(1)}, u32[]{:S(2)}, u32[]{:S(2)}) async-start(bf16[8,192,512]{2,1,0:T(8,128)(2,1)} %pad_maximum_fusion), calls=%async_computation.3 | async-start | bytes 3145728 | tf_op jit(solution)/shard_map/all_to_all | solution.py:178
  155.3 29.0 %copy-start.8 = (bf16[512,1024]{1,0:T(8,128)(2,1)S(1)}, bf16[512,1024]{1,0:T(8,128)(2,1)}, u32[]{:S(2)}) copy-start(bf16[512,1024]{1,0:T(8,128)(2,1)} %get-tuple-element.28) | copy-start | bytes 3145732
  155.3 28.9 %collective-permute-start.2 = (bf16[512,1024]{1,0:T(8,128)(2,1)}, bf16[512,1024]{1,0:T(8,128)(2,1)}, u32[]{:S(2)}, u32[]{:S(2)}) collective-permute-start(bf16[512,1024]{1,0:T(8,128)(2,1)} %get-tuple-element.23), channel_id=1, source_target_pairs={{0,64},{64,0},{128,192},{192,128},{256,320},{320,256},{384,448},{4... | collective-permute-start | bytes 3145736 | tf_op jit(solution)/shard_map/ppermute | solution.py:164
  184.3 20.0 %copy-start.1 = (bf16[8,192,512]{2,1,0:T(8,128)(2,1)}, bf16[8,192,512]{2,1,0:T(8,128)(2,1)S(1)}, u32[]{:S(2)}) copy-start(bf16[8,192,512]{2,1,0:T(8,128)(2,1)S(1)} %all-to-all-done.3) | copy-start | bytes 4718596
  187.5 30.5 %all-to-all-start.4 = ((bf16[8,64,1024]{2,1,0:T(8,128)(2,1)}), bf16[8,64,1024]{2,1,0:T(8,128)(2,1)S(1)}, u32[]{:S(2)}, u32[]{:S(2)}) async-start(bf16[8,64,1024]{2,1,0:T(8,128)(2,1)} %bitcast.56), calls=%async_computation.4 | async-start | bytes 2097152 | tf_op jit(solution)/shard_map/all_to_all | solution.py:178
  204.3 1.2 slice-start
  205.6 1.2 copy-start.3
  208.6 9.6 %copy-start.4 = (f32[512,512]{1,0:T(8,128)}, f32[512,512]{1,0:T(8,128)S(1)}, u32[]{:S(2)}) copy-start(f32[512,512]{1,0:T(8,128)S(1)} %fusion.5) | copy-start | bytes 3145732
  217.9 1.2 copy-start.5

commit v3 on v2

--- a/solution.py
+++ b/solution.py
@@ -12,20 +12,39 @@
 HI = lax.Precision.HIGHEST
 
 
-def factor_diag(block):
+def factor_diag(block, group=8):
     lane = lax.broadcasted_iota(jnp.int32, (8, 128), 1)
     sub = lax.broadcasted_iota(jnp.int32, (8, 128), 0)
-    tiles = [block[8 * r:8 * r + 8, :] for r in range(16)]
-    for j in range(128):
+    lane_row = lane[:1]
+    tiles = [block[8 * r : 8 * r + 8, :] for r in range(16)]
+    for j in range(0, 128, group):
         rb, rs = j // 8, j % 8
-        at_j = lane == j
-        colb = jnp.broadcast_to(tiles[rb][:, j:j + 1], (8, 128))
-        row = jnp.where(at_j[:1], 1.0, tiles[rb][rs:rs + 1, :])
-        scaled = jnp.broadcast_to(row * (1.0 / colb[rs:rs + 1, :]), (8, 128))
+        in_group = (lane >= j) & (lane < j + group)
+        col = [
+            [jnp.broadcast_to(tiles[r][:, j + t : j + t + 1], (8, 128)) for r in range(rb, 16)]
+            for t in range(group)
+        ]
+        row = [tiles[rb][rs + t : rs + t + 1, :] for t in range(group)]
+        scaled = []
+        for t in range(group):
+            here = lane_row == j + t
+            inv = 1.0 / col[t][0][rs + t : rs + t + 1, :]
+            unit = jnp.where(here, 1.0, row[t]) * inv
+            for u in range(t + 1, group):
+                ratio = col[u][0][rs + t : rs + t + 1, :] * inv
+                row[u] = jnp.where(here, 0.0, row[u]) - col[t][0][rs + u : rs + u + 1, :] * unit
+                col[u] = [b - a * ratio for a, b in zip(col[t], col[u])]
+            ahead = (lane_row > j + t) & (lane_row < j + group)
+            scaled.append(jnp.broadcast_to(jnp.where(ahead, 0.0, unit), (8, 128)))
         for r in range(rb, 16):
-            col = colb if r == rb else jnp.broadcast_to(tiles[r][:, j:j + 1], (8, 128))
-            new = jnp.where(at_j, 0.0, tiles[r]) - col * scaled
-            tiles[r] = jnp.where(sub > rs, new, tiles[r]) if r == rb else new
+            new = jnp.where(in_group, 0.0, tiles[r])
+            for t in range(group):
+                new = new - col[t][r - rb] * scaled[t]
+            if r == rb:
+                new = jnp.where(sub >= rs + group, new, tiles[r])
+                for t in range(group):
+                    new = jnp.where(sub == rs + t, jnp.broadcast_to(row[t], (8, 128)), new)
+            tiles[r] = new
     full = jnp.concatenate(tiles, axis=0)
     rows = lax.broadcasted_iota(jnp.int32, (128, 128), 0)
     cols = lax.broadcasted_iota(jnp.int32, (128, 128), 1)
@@ -34,27 +53,30 @@
     root = root * (1.5 - 0.5 * (diag * root) * root)
     return jnp.where(cols < rows, full * root, jnp.where(cols == rows, root, 0.0))
 
+
 def chol_steps_kernel(s_ref, b_ref, *, first, end):
+    count = PMAX // BLK
     b_ref[...] = s_ref[...]
-    col_blk = lax.broadcasted_iota(jnp.int32, (128, 512), 1) // 128
-    row_blk = lax.broadcasted_iota(jnp.int32, (512, 512), 0) // 128
-    all_blk = lax.broadcasted_iota(jnp.int32, (512, 512), 1) // 128
-    eye = (lax.broadcasted_iota(jnp.int32, (128, 512), 1) % 128 == lax.broadcasted_iota(jnp.int32, (128, 512), 0)).astype(jnp.float32)
-
-    def step(jb, carry):
-        at = pl.ds(pl.multiple_of(jb * 128, 128), 128)
-        inv = factor_diag(b_ref[at, at])
-        panel = jnp.where(col_blk == jb, eye, b_ref[at, :])
-        panel = jnp.dot(inv, panel, precision=HI, preferred_element_type=jnp.float32)
-        later = jnp.where(col_blk > jb, panel, 0.0)
-        change = lax.dot_general(later, panel, (((0,), (0,)), ((), ())), precision=HI, preferred_element_type=jnp.float32)
-        kept = jnp.where((row_blk > jb) & (all_blk == jb), 0.0, b_ref[...])
-        b_ref[...] = kept - change
-        b_ref[at, :] = panel
-        return carry
-    lax.fori_loop(first, end, step, 0)
-    if end == PMAX // BLK:
-        b_ref[...] = jnp.where(all_blk <= row_blk, b_ref[...], 0.0)
+    rows = lax.broadcasted_iota(jnp.int32, (BLK, BLK), 0)
+    cols = lax.broadcasted_iota(jnp.int32, (BLK, BLK), 1)
+    eye = (rows == cols).astype(jnp.float32)
+    for jb in range(first, end):
+        here, after = slice(jb * BLK, (jb + 1) * BLK), slice((jb + 1) * BLK, PMAX)
+        inv = factor_diag(b_ref[here, here])
+        b_ref[here, here] = eye
+        panel = jnp.dot(inv, b_ref[here, :], precision=HI, preferred_element_type=jnp.float32)
+        b_ref[here, :] = panel
+        if jb + 1 < count:
+            later = panel[:, after]
+            b_ref[after, here] = jnp.zeros((PMAX - after.start, BLK), jnp.float32)
+            change = lax.dot_general(
+                later, panel, (((0,), (0,)), ((), ())), precision=HI, preferred_element_type=jnp.float32
+            )
+            b_ref[after, :] = b_ref[after, :] - change
+    if end == count:
+        for jb in range(count - 1):
+            here, after = slice(jb * BLK, (jb + 1) * BLK), slice((jb + 1) * BLK, PMAX)
+            b_ref[here, after] = jnp.zeros((BLK, PMAX - after.start), jnp.float32)
 
 
 def chol_steps(state, first, end):
@@ -64,7 +86,7 @@
         in_specs=[pl.BlockSpec(memory_space=pltpu.VMEM)],
         out_specs=pl.BlockSpec(memory_space=pltpu.VMEM),
         cost_estimate=pl.CostEstimate(
-            flops=10_000_000_000 * (end - first), bytes_accessed=2_000_000, transcendentals=0
+            flops=6_000_000_000 * (end - first), bytes_accessed=2_000_000, transcendentals=0
         ),
         name="chol_steps",
     )(state)
@@ -207,28 +229,28 @@
         entries.astype(jnp.bfloat16).reshape(per_row, cols, size, PMAX), col_id, 1, keepdims=False
     ).reshape(per_row * size, PMAX)
     pivot_slice = jnp.concatenate([spread_cols[0, :, :PMAX], entry_slice], axis=0)
-    gathered = lax.all_gather(pivot_slice, "row", axis=0)
-    spread_cols, pivot_slice = lax.optimization_barrier((spread_cols, pivot_slice))
+    pivot_copies = jnp.broadcast_to(pivot_slice[None], (rows,) + pivot_slice.shape)
+    spread_cols, pivot_copies = lax.optimization_barrier((spread_cols, pivot_copies))
+    gathered = swap_axis(pivot_copies, "row")
     strip = swap_axis(spread_cols, "col")
 
     pivot_own = expand_pivot(gathered, half_id, position, per, per_row, size)
     top = pivot_own[: PMAX // BLK * size]
     top = add16(top, to_sibling(top, leaves))
-    top_all = lax.all_gather(top, "col", axis=0)
-
     pivot_own, strip, top = lax.optimization_barrier((pivot_own, strip, top))
+    top_copies = jnp.broadcast_to(top[None], (cols,) + top.shape)
     strip = swap_axis(strip, "row")
     pivot_passed = to_sibling(pivot_own, leaves)
+    top_copies, strip = lax.optimization_barrier((top_copies, strip))
+    top_all = swap_axis(top_copies, "col")
+    main_own, main_other = expand_rows(strip, half_id, position, per, size)
+    main_passed = to_sibling(main_other, leaves)
 
     pivot_mask = jnp.arange(PMAX, dtype=jnp.int32) < pivots
     square = swap_slices(top_all, PMAX // BLK, size).astype(jnp.float32)
     square = jnp.where(
         pivot_mask[:, None] & pivot_mask[None, :], square, jnp.eye(PMAX, dtype=jnp.float32)
     )
-    state = chol_steps(square, 0, 2)
-
-    strip, pivot_passed, state = lax.optimization_barrier((strip, pivot_passed, state))
-    main_own, main_other = expand_rows(strip, half_id, position, per, size)
 
     pivot_cols = add16(pivot_own, pivot_passed)
     own_slice = lax.dynamic_slice_in_dim(
@@ -237,18 +259,21 @@
     far_slices = pivot_cols.reshape(cols, per_col * size, PMAX)
     own_slices = jnp.broadcast_to(own_slice[None], (cols,) + own_slice.shape)
     sent = jnp.concatenate([far_slices, own_slices], axis=1)
-    main_other, sent, state = lax.optimization_barrier((main_other, sent, state))
-    main_passed = to_sibling(main_other, leaves)
+    sent, square = lax.optimization_barrier((sent, square))
     moved = swap_axis(sent, "col")
-    inverse = chol_steps(state, 2, 4)
-    main_passed, moved, inverse = lax.optimization_barrier((main_passed, moved, inverse))
+
+    state = chol_steps(square, 0, 3)
+    main_passed, moved, state = lax.optimization_barrier((main_passed, moved, state))
+    main = add16(main_own, main_passed).reshape(rows, per_row * size, range_cols)
+    main, state = lax.optimization_barrier((main, state))
+    main = swap_axis(main, "row")
+    inverse = chol_steps(state, 3, 4)
     far_cols = swap_slices(moved[:, : per_col * size], per_col, size).astype(jnp.float32)
     own_cols = swap_slices(moved[:, per_col * size :], per_row, size).astype(jnp.float32)
     own_cols = jnp.where(pivot_mask[None, :], own_cols, 0.0)
     far_cols = jnp.where(pivot_mask[None, :], far_cols, 0.0)
 
-    main = add16(main_own, main_passed).reshape(rows, per_row * size, range_cols)
-    assembled = swap_slices(swap_axis(main, "row"), per_row, size).astype(jnp.float32)
+    assembled = swap_slices(main, per_row, size).astype(jnp.float32)
 
     last = (((1,), (1,)), ((), ()))
     factor = lax.dot_general(own_cols, inverse, last, precision=HI, preferred_element_type=jnp.float32)

time: 222 us -> 183 us (0.82)
  blocking collectives: 64.3 us -> 15.3 us
  waiting for transfers between devices: 14.9 us -> 53.7 us
  Pallas kernels: 62 us -> 29.4 us
    all_gather x2 -> x0, blocking collectives: 64.3 us -> none  [the longest x1 40.9 us: on_device(): gathered = lax.all_gather(pivot_slice, 'row', axis=0)]
    pallas_call x2, Pallas kernels: 53.3 us -> 20.8 us  [chol_steps(): pl.pallas_call(functools.partial(chol_steps_kernel, first=first, end=end)...]
    all_to_all x5 -> x6, waiting for transfers between devices: 13.9 us -> 36.2 us  [swap_axis(): return lax.all_to_all(x, axis, 0, 0, tiled=True)]
    ppermute x3, waiting for transfers between devices: 1 us -> 17.5 us  [to_sibling(): return lax.ppermute(x, 'leaf', [(i, i ^ 1) for i in range(leaves)])]
    all_to_all x0 -> x1, blocking collectives: none -> 15.3 us  [swap_axis(): return lax.all_to_all(x, axis, 0, 0, tiled=True)]
    all_to_all x5 -> x6, starting transfers between devices: 39 us -> 41.2 us  [swap_axis(): return lax.all_to_all(x, axis, 0, 0, tiled=True)]
  transfers between devices with their start and end apart: 8 -> 9, of which waited for: 4 -> 8; matrix products, arithmetic and copies ran while one was open for 7% -> 10% of each run, Pallas kernels for 26% -> 15%
where the time goes in v3:
time: 183 us; the launch traced here: 180 us
  waiting for transfers between devices  53.7 us (29%)
  starting transfers between devices  50 us (27%)
  Pallas kernels  29.4 us (16%)
  blocking collectives  15.3 us (8%)
  other arithmetic  11.4 us (6%)
  local copies, waits for them, and re-layouts  10.1 us (6%)
  matrix products  9.28 us (5%)
    all_to_all x6, starting transfers between devices, swap_axis(): return lax.all_to_all(x, axis, 0, 0, tiled=True)  41.2 us
    all_to_all x6, waiting for transfers between devices, swap_axis(): return lax.all_to_all(x, axis, 0, 0, tiled=True)  36.2 us
    pallas_call x2, Pallas kernels, chol_steps(): pl.pallas_call(functools.partial(chol_steps_kernel, first=first, end=end)...  20.8 us
    ppermute x3, waiting for transfers between devices, to_sibling(): return lax.ppermute(x, 'leaf', [(i, i ^ 1) for i in range(leaves)])  17.5 us
    all_to_all x1, blocking collectives, swap_axis(): return lax.all_to_all(x, axis, 0, 0, tiled=True)  15.3 us
    ppermute x3, starting transfers between devices, to_sibling(): return lax.ppermute(x, 'leaf', [(i, i ^ 1) for i in range(leaves)])  8.84 us
    convert_element_type x3, other arithmetic, add16(): return (a.astype(jnp.float32) + b.astype(jnp.float32)).astype(jnp.bfloat16)  4.36 us
    dot_general x1, matrix products, on_device(): lax.dot_general(own_cols, inverse, last, precision=HI, preferred_element_...  4.06 us
  transfers between devices with their start and end apart: 9, of which 8 were waited for; matrix products, arithmetic and copies ran while one was open for 10% of the time, Pallas kernels for 15%

profile of v3, /device:TPU:1, one launch (start us, length us, event | category | flops | bytes accessed | tf_op | source)
XLA Modules:
  0.0 180.1 jit_solution(5657639599910019150)
XLA Ops:
  0.6 0.0 copy-start
  0.6 1.7 copy.13
  2.4 10.2 %all-to-all-start = ((bf16[8,48,384]{2,1,0:T(8,128)(2,1)}), bf16[8,48,384]{2,1,0:T(8,128)(2,1)S(1)}, u32[]{:S(2)}, u32[]{:S(2)}) async-start(bf16[8,48,384]{2,1,0:T(8,128)(2,1)} %bitcast.5), calls=%async_computation | async-start | bytes 589824 | tf_op jit(solution)/shard_map/all_to_all | solution.py:200
  12.5 1.3 convert_element_type.94
  13.8 0.0 copy-done
  13.9 0.1 select_reduce_fusion
  14.0 0.5 broadcast_add_fusion.pos_ref
  14.5 9.2 %all-to-all-done.x_ref = bf16[8,48,384]{2,1,0:T(8,128)(2,1)S(1)} async-done(((bf16[8,48,384]{2,1,0:T(8,128)(2,1)}), bf16[8,48,384]{2,1,0:T(8,128)(2,1)S(1)}, u32[]{:S(2)}, u32[]{:S(2)}) %all-to-all-start) | async-done | bytes 294944 | tf_op jit(solution)/shard_map/all_to_all | solution.py:200
  23.7 0.7 copy-done.6
  24.4 2.2 %expand_cols.1 = bf16[8,48,1024]{2,1,0:T(8,128)(2,1)} custom-call(s32[64]{0:T(128)} %broadcast_add_fusion.pos_ref, bf16[8,48,384]{2,1,0:T(8,128)(2,1)} %copy-done.6), custom_call_target="tpu_custom_call" | custom-call | bytes 1572864 | tf_op jit(solution)/shard_map/expand_cols/pallas_call | solution.py:113
  26.7 0.8 slice_bitcast_fusion
  27.5 0.1 broadcast_in_dim.80
  27.5 15.3 %all_to_all.35.x_ref = bf16[8,112,512]{2,1,0:T(8,128)(2,1)} all-to-all(bf16[8,112,512]{2,1,0:T(8,128)(2,1)S(1)} %broadcast_in_dim.80), channel_id=1, replica_groups=mesh['leaf'=8,'row'=8,'col'=8] {'row'}, dimensions={0} | all-to-all | bytes 1835008 | tf_op jit(solution)/shard_map/all_to_all | solution.py:200
  42.9 7.1 %all-to-all-start.2 = ((bf16[8,48,1024]{2,1,0:T(8,128)(2,1)}), bf16[8,48,1024]{2,1,0:T(8,128)(2,1)}, u32[]{:S(2)}, u32[]{:S(2)}) async-start(bf16[8,48,1024]{2,1,0:T(8,128)(2,1)} %expand_cols.1), calls=%async_computation.2 | async-start | bytes 1572864 | tf_op jit(solution)/shard_map/all_to_all | solution.py:200
  50.0 3.1 %expand_pivot.1 = bf16[1024,512]{1,0:T(8,128)(2,1)} custom-call(s32[1]{0:T(128)} %bitcast.1.half_ref, s32[64]{0:T(128)} %broadcast_add_fusion.pos_ref, bf16[8,112,512]{2,1,0:T(8,128)(2,1)} %all_to_all.35.x_ref), custom_call_target="tpu_custom_call" | custom-call | bytes 4000000 | tf_op jit(solution)/shard_map/expand_pivot/pallas_call | solution.py:148
  53.1 0.9 slice.17
  54.0 2.8 %collective-permute-start = (bf16[64,512]{1,0:T(8,128)(2,1)S(1)}, bf16[64,512]{1,0:T(8,128)(2,1)S(1)}, u32[]{:S(2)}, u32[]{:S(2)}) collective-permute-start(bf16[64,512]{1,0:T(8,128)(2,1)S(1)} %slice.17), channel_id=1, source_target_pairs={{0,64},{64,0},{128,192},{192,128},{256,320},{320,256},{384,448},{4... | collective-permute-start | bytes 196616 | tf_op jit(solution)/shard_map/ppermute | solution.py:186
  56.9 2.6 %collective-permute-done = bf16[64,512]{1,0:T(8,128)(2,1)S(1)} collective-permute-done((bf16[64,512]{1,0:T(8,128)(2,1)S(1)}, bf16[64,512]{1,0:T(8,128)(2,1)S(1)}, u32[]{:S(2)}, u32[]{:S(2)}) %collective-permute-start) | collective-permute-done | bytes 65568 | tf_op jit(solution)/shard_map/ppermute | solution.py:186
  59.5 0.9 add_convert_fusion.2
  60.4 10.8 %all-to-all-done.2 = bf16[8,48,1024]{2,1,0:T(8,128)(2,1)} async-done(((bf16[8,48,1024]{2,1,0:T(8,128)(2,1)}), bf16[8,48,1024]{2,1,0:T(8,128)(2,1)}, u32[]{:S(2)}, u32[]{:S(2)}) %all-to-all-start.2) | async-done | bytes 786464 | tf_op jit(solution)/shard_map/all_to_all | solution.py:200
  71.2 3.5 %all-to-all-start.3 = ((bf16[8,48,1024]{2,1,0:T(8,128)(2,1)}), bf16[8,48,1024]{2,1,0:T(8,128)(2,1)S(1)}, u32[]{:S(2)}, u32[]{:S(2)}) async-start(bf16[8,48,1024]{2,1,0:T(8,128)(2,1)} %all-to-all-done.2), calls=%async_computation.3 | async-start | bytes 1572864 | tf_op jit(solution)/shard_map/all_to_all | solution.py:200
  74.8 2.8 %collective-permute-start.2 = (bf16[1024,512]{1,0:T(8,128)(2,1)}, bf16[1024,512]{1,0:T(8,128)(2,1)S(1)}, u32[]{:S(2)}, u32[]{:S(2)}) collective-permute-start(bf16[1024,512]{1,0:T(8,128)(2,1)} %expand_pivot.1), channel_id=1, source_target_pairs={{0,64},{64,0},{128,192},{192,128},{256,320},{320,256},{384,448},{4... | collective-permute-start | bytes 3145736 | tf_op jit(solution)/shard_map/ppermute | solution.py:186
  77.6 5.8 %all-to-all-done.3.x_ref = bf16[8,48,1024]{2,1,0:T(8,128)(2,1)S(1)} async-done(((bf16[8,48,1024]{2,1,0:T(8,128)(2,1)}), bf16[8,48,1024]{2,1,0:T(8,128)(2,1)S(1)}, u32[]{:S(2)}, u32[]{:S(2)}) %all-to-all-start.3) | async-done | bytes 786464 | tf_op jit(solution)/shard_map/all_to_all | solution.py:200
  83.5 0.9 broadcast_in_dim.81
  84.4 7.9 %all-to-all-start.4 = ((bf16[8,64,512]{2,1,0:T(8,128)(2,1)}), bf16[8,64,512]{2,1,0:T(8,128)(2,1)S(1)}, u32[]{:S(2)}, u32[]{:S(2)}) async-start(bf16[8,64,512]{2,1,0:T(8,128)(2,1)} %broadcast_in_dim.81), calls=%async_computation.4 | async-start | bytes 1048576 | tf_op jit(solution)/shard_map/all_to_all | solution.py:200
  92.3 0.0 copy-done.8
  92.3 0.7 dynamic_slice.13
  93.0 0.7 iota_compare_fusion.2
  93.7 5.7 %collective-permute-done.2 = bf16[1024,512]{1,0:T(8,128)(2,1)S(1)} collective-permute-done((bf16[1024,512]{1,0:T(8,128)(2,1)}, bf16[1024,512]{1,0:T(8,128)(2,1)S(1)}, u32[]{:S(2)}, u32[]{:S(2)}) %collective-permute-start.2) | collective-permute-done | bytes 1048608 | tf_op jit(solution)/shard_map/ppermute | solution.py:186
  99.4 0.0 copy-done.2
  99.4 0.3 add_convert_fusion.1
  99.7 0.0 copy-done.5
  99.8 1.3 pad_maximum_fusion
  101.1 4.9 %all-to-all-done.4 = bf16[8,64,512]{2,1,0:T(8,128)(2,1)S(1)} async-done(((bf16[8,64,512]{2,1,0:T(8,128)(2,1)}), bf16[8,64,512]{2,1,0:T(8,128)(2,1)S(1)}, u32[]{:S(2)}, u32[]{:S(2)}) %all-to-all-start.4) | async-done | bytes 524320 | tf_op jit(solution)/shard_map/all_to_all | solution.py:200
  106.0 0.1 convert_bitcast_fusion.1
  106.1 0.1 copy.14
  106.2 1.2 bitcast_select_fusion.2.s_ref
  107.4 8.0 %all-to-all-start.5 = ((bf16[8,192,512]{2,1,0:T(8,128)(2,1)}), bf16[8,192,512]{2,1,0:T(8,128)(2,1)S(1)}, u32[]{:S(2)}, u32[]{:S(2)}) async-start(bf16[8,192,512]{2,1,0:T(8,128)(2,1)} %pad_maximum_fusion), calls=%async_computation.5 | async-start | bytes 3145728 | tf_op jit(solution)/shard_map/all_to_all | solution.py:200
  115.4 0.7 add_compare_fusion.1
  116.1 0.7 add_compare_fusion
  116.8 3.3 %expand_rows.1 = (bf16[512,1024]{1,0:T(8,128)(2,1)}, bf16[512,1024]{1,0:T(8,128)(2,1)}) custom-call(s32[1]{0:T(128)} %bitcast.1.half_ref, s32[64]{0:T(128)} %broadcast_add_fusion.pos_ref, bf16[8,48,1024]{2,1,0:T(8,128)(2,1)} %copy-done.5), custom_call_target="tpu_custom_call" | custom-call | bytes 6000000 | tf_op jit(solution)/shard_map/expand_rows/pallas_call | solution.py:175
  120.1 3.2 %collective-permute-start.1 = (bf16[512,1024]{1,0:T(8,128)(2,1)}, bf16[512,1024]{1,0:T(8,128)(2,1)}, u32[]{:S(2)}, u32[]{:S(2)}) collective-permute-start(bf16[512,1024]{1,0:T(8,128)(2,1)} %get-tuple-element.23), channel_id=1, source_target_pairs={{0,64},{64,0},{128,192},{192,128},{256,320},{320,256},{384,448},{4... | collective-permute-start | bytes 3145736 | tf_op jit(solution)/shard_map/ppermute | solution.py:186
  123.2 14.7 %chol_steps.2.s_ref = f32[512,512]{1,0:T(8,128)} custom-call(f32[512,512]{1,0:T(8,128)} %bitcast_select_fusion.2.s_ref), custom_call_target="tpu_custom_call" | custom-call | flops 17999998976 | bytes 2000000 | tf_op jit(solution)/shard_map/chol_steps/pallas_call | solution.py:83
  137.9 9.1 %collective-permute-done.1 = bf16[512,1024]{1,0:T(8,128)(2,1)} collective-permute-done((bf16[512,1024]{1,0:T(8,128)(2,1)}, bf16[512,1024]{1,0:T(8,128)(2,1)}, u32[]{:S(2)}, u32[]{:S(2)}) %collective-permute-start.1) | collective-permute-done | bytes 1048608 | tf_op jit(solution)/shard_map/ppermute | solution.py:186
  147.0 5.4 %all-to-all-done.5 = bf16[8,192,512]{2,1,0:T(8,128)(2,1)S(1)} async-done(((bf16[8,192,512]{2,1,0:T(8,128)(2,1)}), bf16[8,192,512]{2,1,0:T(8,128)(2,1)S(1)}, u32[]{:S(2)}, u32[]{:S(2)}) %all-to-all-start.5) | async-done | bytes 1572896 | tf_op jit(solution)/shard_map/all_to_all | solution.py:200
  152.4 0.0 copy-done.7
  152.4 3.2 %add_convert_fusion = bf16[512,1024]{1,0:T(8,128)(2,1)} fusion(bf16[512,1024]{1,0:T(8,128)(2,1)} %collective-permute-done.1, bf16[512,1024]{1,0:T(8,128)(2,1)S(1)} %copy-done.7), kind=kLoop, calls=%fused_computation.4 | loop fusion | flops 2097152 | bytes 3145728 | tf_op jit(solution)/shard_map/convert_element_type | solution.py:190
  155.6 4.5 %all-to-all-start.6 = ((bf16[8,64,1024]{2,1,0:T(8,128)(2,1)}), bf16[8,64,1024]{2,1,0:T(8,128)(2,1)}, u32[]{:S(2)}, u32[]{:S(2)}) async-start(bf16[8,64,1024]{2,1,0:T(8,128)(2,1)} %bitcast.16), calls=%async_computation.6 | async-start | bytes 2097152 | tf_op jit(solution)/shard_map/all_to_all | solution.py:200
  160.2 0.1 convert_bitcast_fusion
  160.3 0.0 copy-done.1
  160.3 0.0 slice-start
  160.3 0.1 copy.15
  160.4 1.1 slice-done
  161.5 0.3 copy.17
  161.8 0.1 bitcast_select_fusion.1
  161.9 6.1 %chol_steps.3 = f32[512,512]{1,0:T(8,128)} custom-call(f32[512,512]{1,0:T(8,128)} %chol_steps.2.s_ref), custom_call_target="tpu_custom_call" | custom-call | flops 6000000000 | bytes 2000000 | tf_op jit(solution)/shard_map/chol_steps/pallas_call | solution.py:83
  168.0 4.1 %fusion.5 = f32[512,512]{1,0:T(8,128)} fusion(f32[512,512]{1,0:T(8,128)S(1)} %bitcast_select_fusion.1, f32[512,512]{1,0:T(8,128)} %chol_steps.3), kind=kOutput, calls=%fused_computation.29 | convolution fusion | flops 1610612736 | bytes 3145728 | tf_op jit(solution)/shard_map/dot_general | solution.py:279
  172.1 0.2 bitcast_select_fusion
  172.3 1.0 copy-done.4
  173.3 3.5 %convolution_convert_fusion = bf16[1024,512]{1,0:T(8,128)(2,1)S(1)} fusion(f32[1024,512]{1,0:T(8,128)S(1)} %bitcast_select_fusion, f32[512,512]{1,0:T(8,128)S(1)} %copy-done.4), kind=kOutput, calls=%fused_computation.7 | convolution fusion | flops 3221749760 | bytes 4194304 | tf_op jit(solution)/shard_map/dot_general | solution.py:280
  176.8 0.0 copy-start.3
  176.8 0.0 all-to-all-done.6
  176.8 1.5 copy.16
  178.4 1.8 fusion.2
  (15 shorter events, 0.1 us)
Async XLA Ops:
  0.6 13.2 %copy-start = (s32[8,24]{1,0:T(8,128)S(1)}, s32[8,24]{1,0:T(8,128)}, u32[]{:S(2)}) copy-start(s32[8,24]{1,0:T(8,128)} %param.5) | copy-start | bytes 2308
  2.4 21.3 %all-to-all-start = ((bf16[8,48,384]{2,1,0:T(8,128)(2,1)}), bf16[8,48,384]{2,1,0:T(8,128)(2,1)S(1)}, u32[]{:S(2)}, u32[]{:S(2)}) async-start(bf16[8,48,384]{2,1,0:T(8,128)(2,1)} %bitcast.5), calls=%async_computation | async-start | bytes 589824 | tf_op jit(solution)/shard_map/all_to_all | solution.py:200
  23.7 0.7 copy-start.6
  42.9 28.4 %all-to-all-start.2 = ((bf16[8,48,1024]{2,1,0:T(8,128)(2,1)}), bf16[8,48,1024]{2,1,0:T(8,128)(2,1)}, u32[]{:S(2)}, u32[]{:S(2)}) async-start(bf16[8,48,1024]{2,1,0:T(8,128)(2,1)} %expand_cols.1), calls=%async_computation.2 | async-start | bytes 1572864 | tf_op jit(solution)/shard_map/all_to_all | solution.py:200
  53.1 39.2 %copy-start.8 = (s32[4]{0:T(128)S(1)}, s32[4]{0:T(128)}, u32[]{:S(2)}) copy-start(s32[4]{0:T(128)} %param.7) | copy-start | bytes 52
  53.1 46.3 %copy-start.2 = (bf16[1024,512]{1,0:T(8,128)(2,1)S(1)}, bf16[1024,512]{1,0:T(8,128)(2,1)}, u32[]{:S(2)}) copy-start(bf16[1024,512]{1,0:T(8,128)(2,1)} %expand_pivot.1) | copy-start | bytes 3145732
  54.0 5.5 %collective-permute-start = (bf16[64,512]{1,0:T(8,128)(2,1)S(1)}, bf16[64,512]{1,0:T(8,128)(2,1)S(1)}, u32[]{:S(2)}, u32[]{:S(2)}) collective-permute-start(bf16[64,512]{1,0:T(8,128)(2,1)S(1)} %slice.17), channel_id=1, source_target_pairs={{0,64},{64,0},{128,192},{192,128},{256,320},{320,256},{384,448},{4... | collective-permute-start | bytes 196616 | tf_op jit(solution)/shard_map/ppermute | solution.py:186
  71.2 12.3 %all-to-all-start.3 = ((bf16[8,48,1024]{2,1,0:T(8,128)(2,1)}), bf16[8,48,1024]{2,1,0:T(8,128)(2,1)S(1)}, u32[]{:S(2)}, u32[]{:S(2)}) async-start(bf16[8,48,1024]{2,1,0:T(8,128)(2,1)} %all-to-all-done.2), calls=%async_computation.3 | async-start | bytes 1572864 | tf_op jit(solution)/shard_map/all_to_all | solution.py:200
  74.8 24.6 %collective-permute-start.2 = (bf16[1024,512]{1,0:T(8,128)(2,1)}, bf16[1024,512]{1,0:T(8,128)(2,1)S(1)}, u32[]{:S(2)}, u32[]{:S(2)}) collective-permute-start(bf16[1024,512]{1,0:T(8,128)(2,1)} %expand_pivot.1), channel_id=1, source_target_pairs={{0,64},{64,0},{128,192},{192,128},{256,320},{320,256},{384,448},{4... | collective-permute-start | bytes 3145736 | tf_op jit(solution)/shard_map/ppermute | solution.py:186
  83.5 16.2 %copy-start.5 = (bf16[8,48,1024]{2,1,0:T(8,128)(2,1)}, bf16[8,48,1024]{2,1,0:T(8,128)(2,1)S(1)}, u32[]{:S(2)}) copy-start(bf16[8,48,1024]{2,1,0:T(8,128)(2,1)S(1)} %all-to-all-done.3.x_ref) | copy-start | bytes 2359300
  84.4 21.6 %all-to-all-start.4 = ((bf16[8,64,512]{2,1,0:T(8,128)(2,1)}), bf16[8,64,512]{2,1,0:T(8,128)(2,1)S(1)}, u32[]{:S(2)}, u32[]{:S(2)}) async-start(bf16[8,64,512]{2,1,0:T(8,128)(2,1)} %broadcast_in_dim.81), calls=%async_computation.4 | async-start | bytes 1048576 | tf_op jit(solution)/shard_map/all_to_all | solution.py:200
  107.4 45.0 %all-to-all-start.5 = ((bf16[8,192,512]{2,1,0:T(8,128)(2,1)}), bf16[8,192,512]{2,1,0:T(8,128)(2,1)S(1)}, u32[]{:S(2)}, u32[]{:S(2)}) async-start(bf16[8,192,512]{2,1,0:T(8,128)(2,1)} %pad_maximum_fusion), calls=%async_computation.5 | async-start | bytes 3145728 | tf_op jit(solution)/shard_map/all_to_all | solution.py:200
  120.1 32.4 %copy-start.7 = (bf16[512,1024]{1,0:T(8,128)(2,1)S(1)}, bf16[512,1024]{1,0:T(8,128)(2,1)}, u32[]{:S(2)}) copy-start(bf16[512,1024]{1,0:T(8,128)(2,1)} %get-tuple-element.29) | copy-start | bytes 3145732
  120.1 26.9 %collective-permute-start.1 = (bf16[512,1024]{1,0:T(8,128)(2,1)}, bf16[512,1024]{1,0:T(8,128)(2,1)}, u32[]{:S(2)}, u32[]{:S(2)}) collective-permute-start(bf16[512,1024]{1,0:T(8,128)(2,1)} %get-tuple-element.23), channel_id=1, source_target_pairs={{0,64},{64,0},{128,192},{192,128},{256,320},{320,256},{384,448},{4... | collective-permute-start | bytes 3145736 | tf_op jit(solution)/shard_map/ppermute | solution.py:186
  152.4 7.8 %copy-start.1 = (bf16[8,192,512]{2,1,0:T(8,128)(2,1)}, bf16[8,192,512]{2,1,0:T(8,128)(2,1)S(1)}, u32[]{:S(2)}) copy-start(bf16[8,192,512]{2,1,0:T(8,128)(2,1)S(1)} %all-to-all-done.5) | copy-start | bytes 4718596
  155.6 21.2 %all-to-all-start.6 = ((bf16[8,64,1024]{2,1,0:T(8,128)(2,1)}), bf16[8,64,1024]{2,1,0:T(8,128)(2,1)}, u32[]{:S(2)}, u32[]{:S(2)}) async-start(bf16[8,64,1024]{2,1,0:T(8,128)(2,1)} %bitcast.16), calls=%async_computation.6 | async-start | bytes 2097152 | tf_op jit(solution)/shard_map/all_to_all | solution.py:200
  160.3 1.2 slice-start
  172.1 1.2 copy-start.4
  176.8 1.6 copy-start.3

commit v4 on v3

--- a/solution.py
+++ b/solution.py
@@ -235,16 +235,19 @@
     strip = swap_axis(spread_cols, "col")
 
     pivot_own = expand_pivot(gathered, half_id, position, per, per_row, size)
-    top = pivot_own[: PMAX // BLK * size]
-    top = add16(top, to_sibling(top, leaves))
-    pivot_own, strip, top = lax.optimization_barrier((pivot_own, strip, top))
-    top_copies = jnp.broadcast_to(top[None], (cols,) + top.shape)
+    top_rows = PMAX // BLK * size
+    row_slice = functools.partial(lax.dynamic_slice_in_dim, pivot_own, slice_size=per_row * size)
+    own_at = (half_id * half_blocks + row_id * per_row) * size
+    other_at = ((1 - half_id) * half_blocks + row_id * per_row) * size
+    mine = jnp.concatenate([pivot_own[:top_rows], row_slice(own_at)], axis=0)
+    theirs = jnp.concatenate([pivot_own[:top_rows], row_slice(other_at)], axis=0)
+    theirs, pivot_own = lax.optimization_barrier((theirs, pivot_own))
+    both = add16(mine, to_sibling(theirs, leaves))
+    pivot_passed = to_sibling(pivot_own, leaves)
+    strip, both = lax.optimization_barrier((strip, both))
     strip = swap_axis(strip, "row")
-    pivot_passed = to_sibling(pivot_own, leaves)
-    top_copies, strip = lax.optimization_barrier((top_copies, strip))
-    top_all = swap_axis(top_copies, "col")
-    main_own, main_other = expand_rows(strip, half_id, position, per, size)
-    main_passed = to_sibling(main_other, leaves)
+    top_all = lax.all_gather(both[:top_rows], "col", axis=0)
+    strip, top_all = lax.optimization_barrier((strip, top_all))
 
     pivot_mask = jnp.arange(PMAX, dtype=jnp.int32) < pivots
     square = swap_slices(top_all, PMAX // BLK, size).astype(jnp.float32)
@@ -253,23 +256,22 @@
     )
 
     pivot_cols = add16(pivot_own, pivot_passed)
-    own_slice = lax.dynamic_slice_in_dim(
-        pivot_cols, (half_id * half_blocks + row_id * per_row) * size, per_row * size
-    )
-    far_slices = pivot_cols.reshape(cols, per_col * size, PMAX)
-    own_slices = jnp.broadcast_to(own_slice[None], (cols,) + own_slice.shape)
-    sent = jnp.concatenate([far_slices, own_slices], axis=1)
-    sent, square = lax.optimization_barrier((sent, square))
+    sent = pivot_cols.reshape(cols, per_col * size, PMAX)
     moved = swap_axis(sent, "col")
+    main_own, main_other = expand_rows(strip, half_id, position, per, size)
+    main_other, square = lax.optimization_barrier((main_other, square))
+    main_passed = to_sibling(main_other, leaves)
 
     state = chol_steps(square, 0, 3)
-    main_passed, moved, state = lax.optimization_barrier((main_passed, moved, state))
+    own_slice, state = lax.optimization_barrier((both[top_rows:], state))
+    own_all = lax.all_gather(own_slice, "col", axis=0)
+    main_passed, moved, own_all, state = lax.optimization_barrier((main_passed, moved, own_all, state))
     main = add16(main_own, main_passed).reshape(rows, per_row * size, range_cols)
     main, state = lax.optimization_barrier((main, state))
     main = swap_axis(main, "row")
     inverse = chol_steps(state, 3, 4)
-    far_cols = swap_slices(moved[:, : per_col * size], per_col, size).astype(jnp.float32)
-    own_cols = swap_slices(moved[:, per_col * size :], per_row, size).astype(jnp.float32)
+    far_cols = swap_slices(moved, per_col, size).astype(jnp.float32)
+    own_cols = swap_slices(own_all, per_row, size).astype(jnp.float32)
     own_cols = jnp.where(pivot_mask[None, :], own_cols, 0.0)
     far_cols = jnp.where(pivot_mask[None, :], far_cols, 0.0)
 

time: 183 us -> 176 us (0.962)
  blocking collectives: 15.3 us -> 51.2 us
  waiting for transfers between devices: 53.7 us -> 25.1 us
  starting transfers between devices: 50 us -> 41.6 us
  local copies, waits for them, and re-layouts: 10.1 us -> 8.24 us
    all_gather x0 -> x2, blocking collectives: none -> 35.9 us  [the longest x1 18.6 us: on_device(): own_all = lax.all_gather(own_slice, 'col', axis=0)]
    all_to_all x6 -> x5, waiting for transfers between devices: 36.2 us -> 19.4 us  [swap_axis(): return lax.all_to_all(x, axis, 0, 0, tiled=True)]
    ppermute x3, waiting for transfers between devices: 17.5 us -> 5.69 us  [to_sibling(): return lax.ppermute(x, 'leaf', [(i, i ^ 1) for i in range(leaves)])]
    all_to_all x6 -> x5, starting transfers between devices: 41.2 us -> 32.8 us  [swap_axis(): return lax.all_to_all(x, axis, 0, 0, tiled=True)]
    slice x4 -> x1, local copies, waits for them, and re-layouts: 2.08 us -> 0.01 us  [on_device(): own_slice, state = lax.optimization_barrier((both[top_rows:], state))]
  transfers between devices with their start and end apart: 9 -> 8, of which waited for: 8 -> 4; matrix products, arithmetic and copies ran while one was open for 10% -> 10% of each run, Pallas kernels for 15% -> 16%
where the time goes in v4:
time: 176 us; the launch traced here: 175 us
  blocking collectives  51.2 us (29%)
  starting transfers between devices  41.6 us (24%)
  Pallas kernels  29.4 us (17%)
  waiting for transfers between devices  25.1 us (14%)
  other arithmetic  9.72 us (6%)
  matrix products  8.44 us (5%)
  local copies, waits for them, and re-layouts  8.24 us (5%)
    all_to_all x5, starting transfers between devices, swap_axis(): return lax.all_to_all(x, axis, 0, 0, tiled=True)  32.8 us
    pallas_call x2, Pallas kernels, chol_steps(): pl.pallas_call(functools.partial(chol_steps_kernel, first=first, end=end)...  20.8 us
    all_to_all x5, waiting for transfers between devices, swap_axis(): return lax.all_to_all(x, axis, 0, 0, tiled=True)  19.4 us
    all_gather x1, blocking collectives, on_device(): own_all = lax.all_gather(own_slice, 'col', axis=0)  18.6 us
    all_gather x1, blocking collectives, on_device(): top_all = lax.all_gather(both[:top_rows], 'col', axis=0)  17.3 us
    all_to_all x1, blocking collectives, swap_axis(): return lax.all_to_all(x, axis, 0, 0, tiled=True)  15.3 us
    ppermute x3, starting transfers between devices, to_sibling(): return lax.ppermute(x, 'leaf', [(i, i ^ 1) for i in range(leaves)])  8.85 us
    ppermute x3, waiting for transfers between devices, to_sibling(): return lax.ppermute(x, 'leaf', [(i, i ^ 1) for i in range(leaves)])  5.69 us
  transfers between devices with their start and end apart: 8, of which 4 were waited for; matrix products, arithmetic and copies ran while one was open for 10% of the time, Pallas kernels for 16%

profile of v4, /device:TPU:1, one launch (start us, length us, event | category | flops | bytes accessed | tf_op | source)
XLA Modules:
  0.0 174.6 jit_solution(13551619727864808020)
XLA Ops:
  0.6 0.0 copy-start
  0.6 1.7 copy.17
  2.4 10.2 %all-to-all-start = ((bf16[8,48,384]{2,1,0:T(8,128)(2,1)}), bf16[8,48,384]{2,1,0:T(8,128)(2,1)S(1)}, u32[]{:S(2)}, u32[]{:S(2)}) async-start(bf16[8,48,384]{2,1,0:T(8,128)(2,1)} %bitcast.5), calls=%async_computation | async-start | bytes 589824 | tf_op jit(solution)/shard_map/all_to_all | solution.py:200
  12.5 1.3 convert_element_type.94
  13.8 0.0 copy-done
  13.9 0.1 select_reduce_fusion
  14.0 0.5 broadcast_add_fusion.pos_ref
  14.5 9.2 %all-to-all-done.x_ref = bf16[8,48,384]{2,1,0:T(8,128)(2,1)S(1)} async-done(((bf16[8,48,384]{2,1,0:T(8,128)(2,1)}), bf16[8,48,384]{2,1,0:T(8,128)(2,1)S(1)}, u32[]{:S(2)}, u32[]{:S(2)}) %all-to-all-start) | async-done | bytes 294944 | tf_op jit(solution)/shard_map/all_to_all | solution.py:200
  23.7 0.0 copy-start.6
  23.7 0.7 copy-done.6
  24.4 2.2 %expand_cols.1 = bf16[8,48,1024]{2,1,0:T(8,128)(2,1)} custom-call(s32[64]{0:T(128)} %broadcast_add_fusion.pos_ref, bf16[8,48,384]{2,1,0:T(8,128)(2,1)} %copy-done.6), custom_call_target="tpu_custom_call" | custom-call | bytes 1572864 | tf_op jit(solution)/shard_map/expand_cols/pallas_call | solution.py:113
  26.7 0.8 slice_bitcast_fusion
  27.5 0.1 broadcast_in_dim.68
  27.5 15.3 %all_to_all.30.x_ref = bf16[8,112,512]{2,1,0:T(8,128)(2,1)} all-to-all(bf16[8,112,512]{2,1,0:T(8,128)(2,1)S(1)} %broadcast_in_dim.68), channel_id=1, replica_groups=mesh['leaf'=8,'row'=8,'col'=8] {'row'}, dimensions={0} | all-to-all | bytes 1835008 | tf_op jit(solution)/shard_map/all_to_all | solution.py:200
  42.9 7.1 %all-to-all-start.1 = ((bf16[8,48,1024]{2,1,0:T(8,128)(2,1)}), bf16[8,48,1024]{2,1,0:T(8,128)(2,1)}, u32[]{:S(2)}, u32[]{:S(2)}) async-start(bf16[8,48,1024]{2,1,0:T(8,128)(2,1)} %expand_cols.1), calls=%async_computation.1 | async-start | bytes 1572864 | tf_op jit(solution)/shard_map/all_to_all | solution.py:200
  50.0 0.0 copy-start.8
  50.0 3.1 %expand_pivot.1 = bf16[1024,512]{1,0:T(8,128)(2,1)} custom-call(s32[1]{0:T(128)} %bitcast.1.half_ref, s32[64]{0:T(128)} %broadcast_add_fusion.pos_ref, bf16[8,112,512]{2,1,0:T(8,128)(2,1)} %all_to_all.30.x_ref), custom_call_target="tpu_custom_call" | custom-call | bytes 4000000 | tf_op jit(solution)/shard_map/expand_pivot/pallas_call | solution.py:148
  53.1 1.0 constant_dynamic-slice_fusion
  54.1 2.9 %collective-permute-start = (bf16[128,512]{1,0:T(8,128)(2,1)S(1)}, bf16[128,512]{1,0:T(8,128)(2,1)S(1)}, u32[]{:S(2)}, u32[]{:S(2)}) collective-permute-start(bf16[128,512]{1,0:T(8,128)(2,1)S(1)} %pad_maximum_fusion), channel_id=1, source_target_pairs={{0,64},{64,0},{128,192},{192,128},{256,320},{320,256},{384,448},{4... | collective-permute-start | bytes 393224 | tf_op jit(solution)/shard_map/ppermute | solution.py:186
  57.0 4.0 %collective-permute-done = bf16[128,512]{1,0:T(8,128)(2,1)S(1)} collective-permute-done((bf16[128,512]{1,0:T(8,128)(2,1)S(1)}, bf16[128,512]{1,0:T(8,128)(2,1)S(1)}, u32[]{:S(2)}, u32[]{:S(2)}) %collective-permute-start) | collective-permute-done | bytes 131104 | tf_op jit(solution)/shard_map/ppermute | solution.py:186
  61.1 10.2 %all-to-all-done.1 = bf16[8,48,1024]{2,1,0:T(8,128)(2,1)} async-done(((bf16[8,48,1024]{2,1,0:T(8,128)(2,1)}), bf16[8,48,1024]{2,1,0:T(8,128)(2,1)}, u32[]{:S(2)}, u32[]{:S(2)}) %all-to-all-start.1) | async-done | bytes 786464 | tf_op jit(solution)/shard_map/all_to_all | solution.py:200
  71.2 3.5 %all-to-all-start.3 = ((bf16[8,48,1024]{2,1,0:T(8,128)(2,1)}), bf16[8,48,1024]{2,1,0:T(8,128)(2,1)S(1)}, u32[]{:S(2)}, u32[]{:S(2)}) async-start(bf16[8,48,1024]{2,1,0:T(8,128)(2,1)} %all-to-all-done.1), calls=%async_computation.3 | async-start | bytes 1572864 | tf_op jit(solution)/shard_map/all_to_all | solution.py:200
  74.8 0.0 copy-done.2
  74.8 2.8 %collective-permute-start.2 = (bf16[1024,512]{1,0:T(8,128)(2,1)S(1)}, bf16[1024,512]{1,0:T(8,128)(2,1)S(1)}, u32[]{:S(2)}, u32[]{:S(2)}) collective-permute-start(bf16[1024,512]{1,0:T(8,128)(2,1)S(1)} %copy-done.2), channel_id=1, source_target_pairs={{0,64},{64,0},{128,192},{192,128},{256,320},{320,256},{384,448},{4... | collective-permute-start | bytes 3145736 | tf_op jit(solution)/shard_map/ppermute | solution.py:186
  77.7 0.0 copy-done.8
  77.7 0.6 dynamic_slice.16
  78.3 0.6 iota_compare_fusion.2
  78.9 0.7 add_compare_fusion.1
  79.6 0.7 add_compare_fusion
  80.3 17.3 %all-gather = bf16[512,512]{1,0:T(8,128)(2,1)S(1)} all-gather(bf16[64,512]{1,0:T(8,128)(2,1)S(1)} %get-tuple-element.46), channel_id=2, replica_groups=mesh['leaf'=8,'row'=8,'col'=8] {'col'}, dimensions={0}, use_global_device_ids=true | all-gather | bytes 589824 | tf_op jit(solution)/shard_map/all_gather | solution.py:249
  97.5 1.7 collective-permute-done.2
  99.2 1.3 add_convert_fusion.1
  100.5 0.0 all-to-all-done.3.x_ref
  100.5 6.5 %all-to-all-start.4 = ((bf16[8,128,512]{2,1,0:T(8,128)(2,1)}), bf16[8,128,512]{2,1,0:T(8,128)(2,1)S(1)}, u32[]{:S(2)}, u32[]{:S(2)}) async-start(bf16[8,128,512]{2,1,0:T(8,128)(2,1)} %bitcast.13), calls=%async_computation.4 | async-start | bytes 2097152 | tf_op jit(solution)/shard_map/all_to_all | solution.py:200
  107.0 0.0 copy-done.5
  107.0 3.3 %expand_rows.1 = (bf16[512,1024]{1,0:T(8,128)(2,1)}, bf16[512,1024]{1,0:T(8,128)(2,1)}) custom-call(s32[1]{0:T(128)} %bitcast.1.half_ref, s32[64]{0:T(128)} %broadcast_add_fusion.pos_ref, bf16[8,48,1024]{2,1,0:T(8,128)(2,1)} %copy-done.5), custom_call_target="tpu_custom_call" | custom-call | bytes 6000000 | tf_op jit(solution)/shard_map/expand_rows/pallas_call | solution.py:175
  110.3 0.1 convert_bitcast_fusion.2
  110.4 0.1 copy.18
  110.6 1.2 bitcast_select_fusion.2.s_ref
  111.7 3.1 %collective-permute-start.1 = (bf16[512,1024]{1,0:T(8,128)(2,1)}, bf16[512,1024]{1,0:T(8,128)(2,1)S(1)}, u32[]{:S(2)}, u32[]{:S(2)}) collective-permute-start(bf16[512,1024]{1,0:T(8,128)(2,1)} %get-tuple-element.30), channel_id=1, source_target_pairs={{0,64},{64,0},{128,192},{192,128},{256,320},{320,256},{384,448},{4... | collective-permute-start | bytes 3145736 | tf_op jit(solution)/shard_map/ppermute | solution.py:186
  114.9 14.7 %chol_steps.2.s_ref = f32[512,512]{1,0:T(8,128)} custom-call(f32[512,512]{1,0:T(8,128)} %bitcast_select_fusion.2.s_ref), custom_call_target="tpu_custom_call" | custom-call | flops 17999998976 | bytes 2000000 | tf_op jit(solution)/shard_map/chol_steps/pallas_call | solution.py:83
  129.6 18.6 %all-gather.1 = bf16[512,512]{1,0:T(8,128)(2,1)} all-gather(bf16[64,512]{1,0:T(8,128)(2,1)S(1)} %get-tuple-element.33), channel_id=3, replica_groups=mesh['leaf'=8,'row'=8,'col'=8] {'col'}, dimensions={0}, use_global_device_ids=true | all-gather | bytes 589824 | tf_op jit(solution)/shard_map/all_gather | solution.py:267
  148.2 0.0 collective-permute-done.1
  148.2 0.0 all-to-all-done.4
  148.2 0.0 copy-done.7
  148.2 1.4 add_convert_fusion
  149.6 0.3 convert_bitcast_fusion
  149.9 5.4 %all-to-all-start.5 = ((bf16[8,64,1024]{2,1,0:T(8,128)(2,1)}), bf16[8,64,1024]{2,1,0:T(8,128)(2,1)S(1)}, u32[]{:S(2)}, u32[]{:S(2)}) async-start(bf16[8,64,1024]{2,1,0:T(8,128)(2,1)} %bitcast.56), calls=%async_computation.5 | async-start | bytes 2097152 | tf_op jit(solution)/shard_map/all_to_all | solution.py:200
  155.3 1.2 convert_bitcast_fusion.1
  156.5 0.1 copy.19
  156.5 1.5 copy.21
  158.1 0.1 bitcast_select_fusion.1
  158.2 6.1 %chol_steps.3 = f32[512,512]{1,0:T(8,128)} custom-call(f32[512,512]{1,0:T(8,128)} %chol_steps.2.s_ref), custom_call_target="tpu_custom_call" | custom-call | flops 6000000000 | bytes 2000000 | tf_op jit(solution)/shard_map/chol_steps/pallas_call | solution.py:83
  164.3 3.2 %fusion.6 = f32[512,512]{1,0:T(8,128)S(1)} fusion(f32[512,512]{1,0:T(8,128)S(1)} %bitcast_select_fusion.1, f32[512,512]{1,0:T(8,128)} %chol_steps.3), kind=kOutput, calls=%fused_computation.33 | convolution fusion | flops 1610612736 | bytes 3145728 | tf_op jit(solution)/shard_map/dot_general | solution.py:281
  167.5 0.0 copy-done.1
  167.5 0.0 copy-start.3
  167.5 0.0 copy-start.4
  167.5 0.2 bitcast_select_fusion
  167.8 1.3 copy-done.4
  169.1 3.5 %convolution_convert_fusion = bf16[1024,512]{1,0:T(8,128)(2,1)S(1)} fusion(f32[1024,512]{1,0:T(8,128)S(1)} %bitcast_select_fusion, f32[512,512]{1,0:T(8,128)S(1)} %copy-done.4), kind=kOutput, calls=%fused_computation.7 | convolution fusion | flops 3221749760 | bytes 4194304 | tf_op jit(solution)/shard_map/dot_general | solution.py:282
  172.6 0.0 all-to-all-done.5
  172.6 0.2 copy.20
  172.9 0.0 copy-done.3
  172.9 1.8 %fusion.2 = bf16[1,512,1024]{2,1,0:T(8,128)(2,1)} fusion(bf16[1024,512]{1,0:T(8,128)(2,1)S(1)} %convolution_convert_fusion, f32[8,4,16,1024]{3,2,0,1:T(8,128)S(1)} %copy.20, pred[1024]{0:T(1024)(128)(4,1)S(1)} %add_compare_fusion, pred[512]{0:T(512)(128)(4,1)S(1)} %add_compare_fusion.1, f32[512,512]{1,0:T(8,128)S(1)} %fusion.6), kind=kOutput, calls=%fused_computation.8 | convolution fusion | flops 539230208 | bytes 5244416 | tf_op jit(solution)/shard_map/dot_general | solution.py:283
  (11 shorter events, 0.1 us)
Async XLA Ops:
  0.6 13.2 %copy-start = (s32[8,24]{1,0:T(8,128)S(1)}, s32[8,24]{1,0:T(8,128)}, u32[]{:S(2)}) copy-start(s32[8,24]{1,0:T(8,128)} %param.5) | copy-start | bytes 2308
  2.4 21.3 %all-to-all-start = ((bf16[8,48,384]{2,1,0:T(8,128)(2,1)}), bf16[8,48,384]{2,1,0:T(8,128)(2,1)S(1)}, u32[]{:S(2)}, u32[]{:S(2)}) async-start(bf16[8,48,384]{2,1,0:T(8,128)(2,1)} %bitcast.5), calls=%async_computation | async-start | bytes 589824 | tf_op jit(solution)/shard_map/all_to_all | solution.py:200
  23.7 0.7 copy-start.6
  42.9 28.4 %all-to-all-start.1 = ((bf16[8,48,1024]{2,1,0:T(8,128)(2,1)}), bf16[8,48,1024]{2,1,0:T(8,128)(2,1)}, u32[]{:S(2)}, u32[]{:S(2)}) async-start(bf16[8,48,1024]{2,1,0:T(8,128)(2,1)} %expand_cols.1), calls=%async_computation.1 | async-start | bytes 1572864 | tf_op jit(solution)/shard_map/all_to_all | solution.py:200
  50.0 27.7 %copy-start.8 = (s32[4]{0:T(128)S(1)}, s32[4]{0:T(128)}, u32[]{:S(2)}) copy-start(s32[4]{0:T(128)} %param.7) | copy-start | bytes 52
  53.1 21.7 %copy-start.2 = (bf16[1024,512]{1,0:T(8,128)(2,1)S(1)}, bf16[1024,512]{1,0:T(8,128)(2,1)}, u32[]{:S(2)}) copy-start(bf16[1024,512]{1,0:T(8,128)(2,1)} %expand_pivot.1) | copy-start | bytes 3145732
  54.1 6.9 %collective-permute-start = (bf16[128,512]{1,0:T(8,128)(2,1)S(1)}, bf16[128,512]{1,0:T(8,128)(2,1)S(1)}, u32[]{:S(2)}, u32[]{:S(2)}) collective-permute-start(bf16[128,512]{1,0:T(8,128)(2,1)S(1)} %pad_maximum_fusion), channel_id=1, source_target_pairs={{0,64},{64,0},{128,192},{192,128},{256,320},{320,256},{384,448},{4... | collective-permute-start | bytes 393224 | tf_op jit(solution)/shard_map/ppermute | solution.py:186
  71.2 29.3 %all-to-all-start.3 = ((bf16[8,48,1024]{2,1,0:T(8,128)(2,1)}), bf16[8,48,1024]{2,1,0:T(8,128)(2,1)S(1)}, u32[]{:S(2)}, u32[]{:S(2)}) async-start(bf16[8,48,1024]{2,1,0:T(8,128)(2,1)} %all-to-all-done.1), calls=%async_computation.3 | async-start | bytes 1572864 | tf_op jit(solution)/shard_map/all_to_all | solution.py:200
  74.8 24.4 %collective-permute-start.2 = (bf16[1024,512]{1,0:T(8,128)(2,1)S(1)}, bf16[1024,512]{1,0:T(8,128)(2,1)S(1)}, u32[]{:S(2)}, u32[]{:S(2)}) collective-permute-start(bf16[1024,512]{1,0:T(8,128)(2,1)S(1)} %copy-done.2), channel_id=1, source_target_pairs={{0,64},{64,0},{128,192},{192,128},{256,320},{320,256},{384,448},{4... | collective-permute-start | bytes 3145736 | tf_op jit(solution)/shard_map/ppermute | solution.py:186
  100.5 6.5 %copy-start.5 = (bf16[8,48,1024]{2,1,0:T(8,128)(2,1)}, bf16[8,48,1024]{2,1,0:T(8,128)(2,1)S(1)}, u32[]{:S(2)}) copy-start(bf16[8,48,1024]{2,1,0:T(8,128)(2,1)S(1)} %all-to-all-done.3.x_ref) | copy-start | bytes 2359300
  100.5 47.6 %all-to-all-start.4 = ((bf16[8,128,512]{2,1,0:T(8,128)(2,1)}), bf16[8,128,512]{2,1,0:T(8,128)(2,1)S(1)}, u32[]{:S(2)}, u32[]{:S(2)}) async-start(bf16[8,128,512]{2,1,0:T(8,128)(2,1)} %bitcast.13), calls=%async_computation.4 | async-start | bytes 2097152 | tf_op jit(solution)/shard_map/all_to_all | solution.py:200
  111.7 36.5 %copy-start.7 = (bf16[512,1024]{1,0:T(8,128)(2,1)S(1)}, bf16[512,1024]{1,0:T(8,128)(2,1)}, u32[]{:S(2)}) copy-start(bf16[512,1024]{1,0:T(8,128)(2,1)} %get-tuple-element.36) | copy-start | bytes 3145732
  111.7 36.5 %collective-permute-start.1 = (bf16[512,1024]{1,0:T(8,128)(2,1)}, bf16[512,1024]{1,0:T(8,128)(2,1)S(1)}, u32[]{:S(2)}, u32[]{:S(2)}) collective-permute-start(bf16[512,1024]{1,0:T(8,128)(2,1)} %get-tuple-element.30), channel_id=1, source_target_pairs={{0,64},{64,0},{128,192},{192,128},{256,320},{320,256},{384,448},{4... | collective-permute-start | bytes 3145736 | tf_op jit(solution)/shard_map/ppermute | solution.py:186
  149.9 22.8 %all-to-all-start.5 = ((bf16[8,64,1024]{2,1,0:T(8,128)(2,1)}), bf16[8,64,1024]{2,1,0:T(8,128)(2,1)S(1)}, u32[]{:S(2)}, u32[]{:S(2)}) async-start(bf16[8,64,1024]{2,1,0:T(8,128)(2,1)} %bitcast.56), calls=%async_computation.5 | async-start | bytes 2097152 | tf_op jit(solution)/shard_map/all_to_all | solution.py:200
  164.3 3.2 %copy-start.1 = (f32[8,8,16,512]{3,2,1,0:T(8,128)S(1)}, f32[8,8,16,512]{3,2,1,0:T(8,128)}, u32[]{:S(2)}) copy-start(f32[8,8,16,512]{3,2,1,0:T(8,128)} %copy.21) | copy-start | bytes 6291460
  167.5 5.3 %copy-start.3 = (f32[512,512]{1,0:T(8,128)}, f32[512,512]{1,0:T(8,128)S(1)}, u32[]{:S(2)}) copy-start(f32[512,512]{1,0:T(8,128)S(1)} %fusion.6) | copy-start | bytes 3145732
  167.5 1.6 copy-start.4

commit v5 on v4

--- a/solution.py
+++ b/solution.py
@@ -244,10 +244,9 @@
     theirs, pivot_own = lax.optimization_barrier((theirs, pivot_own))
     both = add16(mine, to_sibling(theirs, leaves))
     pivot_passed = to_sibling(pivot_own, leaves)
-    strip, both = lax.optimization_barrier((strip, both))
-    strip = swap_axis(strip, "row")
     top_all = lax.all_gather(both[:top_rows], "col", axis=0)
     strip, top_all = lax.optimization_barrier((strip, top_all))
+    strip = swap_axis(strip, "row")
 
     pivot_mask = jnp.arange(PMAX, dtype=jnp.int32) < pivots
     square = swap_slices(top_all, PMAX // BLK, size).astype(jnp.float32)

time: 176 us -> 185 us (1.051)
  waiting for transfers between devices: 25.1 us -> 32.8 us
  blocking collectives: 51.2 us -> 54.8 us
    ppermute x3, waiting for transfers between devices: 5.69 us -> 23.6 us  [to_sibling(): return lax.ppermute(x, 'leaf', [(i, i ^ 1) for i in range(leaves)])]
    all_to_all x5, waiting for transfers between devices: 19.4 us -> 9.21 us  [swap_axis(): return lax.all_to_all(x, axis, 0, 0, tiled=True)]
    all_gather x1, blocking collectives: 17.3 us -> 20.6 us  [on_device(): top_all = lax.all_gather(both[:top_rows], 'col', axis=0)]
  transfers between devices with their start and end apart: 8 -> 8, of which waited for: 4 -> 3; matrix products, arithmetic and copies ran while one was open for 10% -> 10% of each run, Pallas kernels for 16% -> 15%
where the time goes in v5:
time: 185 us; the launch traced here: 184 us
  blocking collectives  54.8 us (30%)
  starting transfers between devices  40.1 us (22%)
  waiting for transfers between devices  32.8 us (18%)
  Pallas kernels  29.4 us (16%)
  other arithmetic  9.72 us (5%)
  matrix products  8.44 us (5%)
  local copies, waits for them, and re-layouts  8.23 us (4%)
    all_to_all x5, starting transfers between devices, swap_axis(): return lax.all_to_all(x, axis, 0, 0, tiled=True)  31.2 us
    ppermute x3, waiting for transfers between devices, to_sibling(): return lax.ppermute(x, 'leaf', [(i, i ^ 1) for i in range(leaves)])  23.6 us
    pallas_call x2, Pallas kernels, chol_steps(): pl.pallas_call(functools.partial(chol_steps_kernel, first=first, end=end)...  20.8 us
    all_gather x1, blocking collectives, on_device(): top_all = lax.all_gather(both[:top_rows], 'col', axis=0)  20.6 us
    all_gather x1, blocking collectives, on_device(): own_all = lax.all_gather(own_slice, 'col', axis=0)  18.9 us
    all_to_all x1, blocking collectives, swap_axis(): return lax.all_to_all(x, axis, 0, 0, tiled=True)  15.3 us
    all_to_all x5, waiting for transfers between devices, swap_axis(): return lax.all_to_all(x, axis, 0, 0, tiled=True)  9.21 us
    ppermute x3, starting transfers between devices, to_sibling(): return lax.ppermute(x, 'leaf', [(i, i ^ 1) for i in range(leaves)])  8.86 us
  transfers between devices with their start and end apart: 8, of which 3 were waited for; matrix products, arithmetic and copies ran while one was open for 10% of the time, Pallas kernels for 15%

profile of v5, /device:TPU:1, one launch (start us, length us, event | category | flops | bytes accessed | tf_op | source)
XLA Modules:
  0.0 184.5 jit_solution(12709369734682499477)
XLA Ops:
  0.6 0.0 copy-start
  0.6 1.7 copy.17
  2.4 10.2 %all-to-all-start = ((bf16[8,48,384]{2,1,0:T(8,128)(2,1)}), bf16[8,48,384]{2,1,0:T(8,128)(2,1)S(1)}, u32[]{:S(2)}, u32[]{:S(2)}) async-start(bf16[8,48,384]{2,1,0:T(8,128)(2,1)} %bitcast.5), calls=%async_computation | async-start | bytes 589824 | tf_op jit(solution)/shard_map/all_to_all | solution.py:200
  12.5 1.3 convert_element_type.94
  13.8 0.0 copy-done
  13.9 0.1 select_reduce_fusion
  14.0 0.5 broadcast_add_fusion.pos_ref
  14.5 9.2 %all-to-all-done.x_ref = bf16[8,48,384]{2,1,0:T(8,128)(2,1)S(1)} async-done(((bf16[8,48,384]{2,1,0:T(8,128)(2,1)}), bf16[8,48,384]{2,1,0:T(8,128)(2,1)S(1)}, u32[]{:S(2)}, u32[]{:S(2)}) %all-to-all-start) | async-done | bytes 294944 | tf_op jit(solution)/shard_map/all_to_all | solution.py:200
  23.7 0.0 copy-start.6
  23.7 0.7 copy-done.6
  24.4 2.2 %expand_cols.1 = bf16[8,48,1024]{2,1,0:T(8,128)(2,1)} custom-call(s32[64]{0:T(128)} %broadcast_add_fusion.pos_ref, bf16[8,48,384]{2,1,0:T(8,128)(2,1)} %copy-done.6), custom_call_target="tpu_custom_call" | custom-call | bytes 1572864 | tf_op jit(solution)/shard_map/expand_cols/pallas_call | solution.py:113
  26.7 0.8 slice_bitcast_fusion
  27.5 0.1 broadcast_in_dim.68
  27.5 15.3 %all_to_all.30.x_ref = bf16[8,112,512]{2,1,0:T(8,128)(2,1)} all-to-all(bf16[8,112,512]{2,1,0:T(8,128)(2,1)S(1)} %broadcast_in_dim.68), channel_id=1, replica_groups=mesh['leaf'=8,'row'=8,'col'=8] {'row'}, dimensions={0} | all-to-all | bytes 1835008 | tf_op jit(solution)/shard_map/all_to_all | solution.py:200
  42.9 7.1 %all-to-all-start.1 = ((bf16[8,48,1024]{2,1,0:T(8,128)(2,1)}), bf16[8,48,1024]{2,1,0:T(8,128)(2,1)}, u32[]{:S(2)}, u32[]{:S(2)}) async-start(bf16[8,48,1024]{2,1,0:T(8,128)(2,1)} %expand_cols.1), calls=%async_computation.1 | async-start | bytes 1572864 | tf_op jit(solution)/shard_map/all_to_all | solution.py:200
  50.0 3.1 %expand_pivot.1 = bf16[1024,512]{1,0:T(8,128)(2,1)} custom-call(s32[1]{0:T(128)} %bitcast.1.half_ref, s32[64]{0:T(128)} %broadcast_add_fusion.pos_ref, bf16[8,112,512]{2,1,0:T(8,128)(2,1)} %all_to_all.30.x_ref), custom_call_target="tpu_custom_call" | custom-call | bytes 4000000 | tf_op jit(solution)/shard_map/expand_pivot/pallas_call | solution.py:148
  53.1 0.0 copy-start.2
  53.1 1.0 constant_dynamic-slice_fusion
  54.1 2.9 %collective-permute-start = (bf16[128,512]{1,0:T(8,128)(2,1)S(1)}, bf16[128,512]{1,0:T(8,128)(2,1)S(1)}, u32[]{:S(2)}, u32[]{:S(2)}) collective-permute-start(bf16[128,512]{1,0:T(8,128)(2,1)S(1)} %pad_maximum_fusion), channel_id=1, source_target_pairs={{0,64},{64,0},{128,192},{192,128},{256,320},{320,256},{384,448},{4... | collective-permute-start | bytes 393224 | tf_op jit(solution)/shard_map/ppermute | solution.py:186
  57.0 4.0 %collective-permute-done = bf16[128,512]{1,0:T(8,128)(2,1)S(1)} collective-permute-done((bf16[128,512]{1,0:T(8,128)(2,1)S(1)}, bf16[128,512]{1,0:T(8,128)(2,1)S(1)}, u32[]{:S(2)}, u32[]{:S(2)}) %collective-permute-start) | collective-permute-done | bytes 131104 | tf_op jit(solution)/shard_map/ppermute | solution.py:186
  61.1 20.6 %all-gather = bf16[512,512]{1,0:T(8,128)(2,1)S(1)} all-gather(bf16[64,512]{1,0:T(8,128)(2,1)S(1)} %get-tuple-element.42), channel_id=2, replica_groups=mesh['leaf'=8,'row'=8,'col'=8] {'col'}, dimensions={0}, use_global_device_ids=true | all-gather | bytes 589824 | tf_op jit(solution)/shard_map/all_gather | solution.py:247
  81.7 0.0 all-to-all-done.1
  81.7 3.5 %all-to-all-start.3 = ((bf16[8,48,1024]{2,1,0:T(8,128)(2,1)}), bf16[8,48,1024]{2,1,0:T(8,128)(2,1)S(1)}, u32[]{:S(2)}, u32[]{:S(2)}) async-start(bf16[8,48,1024]{2,1,0:T(8,128)(2,1)} %all-to-all-done.1), calls=%async_computation.3 | async-start | bytes 1572864 | tf_op jit(solution)/shard_map/all_to_all | solution.py:200
  85.2 0.0 copy-done.2
  85.2 2.9 %collective-permute-start.2 = (bf16[1024,512]{1,0:T(8,128)(2,1)S(1)}, bf16[1024,512]{1,0:T(8,128)(2,1)S(1)}, u32[]{:S(2)}, u32[]{:S(2)}) collective-permute-start(bf16[1024,512]{1,0:T(8,128)(2,1)S(1)} %copy-done.2), channel_id=1, source_target_pairs={{0,64},{64,0},{128,192},{192,128},{256,320},{320,256},{384,448},{4... | collective-permute-start | bytes 3145736 | tf_op jit(solution)/shard_map/ppermute | solution.py:186
  88.1 0.0 copy-done.8
  88.1 0.6 dynamic_slice.16
  88.7 0.6 iota_compare_fusion.2
  89.4 0.7 add_compare_fusion.1
  90.0 0.7 add_compare_fusion
  90.7 0.1 convert_bitcast_fusion.2
  90.8 0.1 copy.18
  90.9 1.2 bitcast_select_fusion.2.s_ref
  92.1 19.6 %collective-permute-done.2 = bf16[1024,512]{1,0:T(8,128)(2,1)S(1)} collective-permute-done((bf16[1024,512]{1,0:T(8,128)(2,1)S(1)}, bf16[1024,512]{1,0:T(8,128)(2,1)S(1)}, u32[]{:S(2)}, u32[]{:S(2)}) %collective-permute-start.2) | collective-permute-done | bytes 1048608 | tf_op jit(solution)/shard_map/ppermute | solution.py:186
  111.7 1.3 add_convert_fusion.1
  113.0 0.0 all-to-all-done.3.x_ref
  113.0 5.3 %all-to-all-start.4 = ((bf16[8,128,512]{2,1,0:T(8,128)(2,1)}), bf16[8,128,512]{2,1,0:T(8,128)(2,1)S(1)}, u32[]{:S(2)}, u32[]{:S(2)}) async-start(bf16[8,128,512]{2,1,0:T(8,128)(2,1)} %bitcast.13), calls=%async_computation.4 | async-start | bytes 2097152 | tf_op jit(solution)/shard_map/all_to_all | solution.py:200
  118.3 0.0 copy-done.5
  118.3 3.3 %expand_rows.1 = (bf16[512,1024]{1,0:T(8,128)(2,1)}, bf16[512,1024]{1,0:T(8,128)(2,1)}) custom-call(s32[1]{0:T(128)} %bitcast.1.half_ref, s32[64]{0:T(128)} %broadcast_add_fusion.pos_ref, bf16[8,48,1024]{2,1,0:T(8,128)(2,1)} %copy-done.5), custom_call_target="tpu_custom_call" | custom-call | bytes 6000000 | tf_op jit(solution)/shard_map/expand_rows/pallas_call | solution.py:175
  121.5 3.2 %collective-permute-start.1 = (bf16[512,1024]{1,0:T(8,128)(2,1)}, bf16[512,1024]{1,0:T(8,128)(2,1)S(1)}, u32[]{:S(2)}, u32[]{:S(2)}) collective-permute-start(bf16[512,1024]{1,0:T(8,128)(2,1)} %get-tuple-element.26), channel_id=1, source_target_pairs={{0,64},{64,0},{128,192},{192,128},{256,320},{320,256},{384,448},{4... | collective-permute-start | bytes 3145736 | tf_op jit(solution)/shard_map/ppermute | solution.py:186
  124.7 14.7 %chol_steps.2.s_ref = f32[512,512]{1,0:T(8,128)} custom-call(f32[512,512]{1,0:T(8,128)} %bitcast_select_fusion.2.s_ref), custom_call_target="tpu_custom_call" | custom-call | flops 17999998976 | bytes 2000000 | tf_op jit(solution)/shard_map/chol_steps/pallas_call | solution.py:83
  139.4 18.9 %all-gather.1 = bf16[512,512]{1,0:T(8,128)(2,1)} all-gather(bf16[64,512]{1,0:T(8,128)(2,1)S(1)} %get-tuple-element.29), channel_id=3, replica_groups=mesh['leaf'=8,'row'=8,'col'=8] {'col'}, dimensions={0}, use_global_device_ids=true | all-gather | bytes 589824 | tf_op jit(solution)/shard_map/all_gather | solution.py:266
  158.3 0.0 collective-permute-done.1
  158.3 0.0 all-to-all-done.4
  158.3 0.0 copy-done.7
  158.3 1.4 add_convert_fusion
  159.7 0.3 convert_bitcast_fusion
  160.0 5.1 %all-to-all-start.5 = ((bf16[8,64,1024]{2,1,0:T(8,128)(2,1)}), bf16[8,64,1024]{2,1,0:T(8,128)(2,1)S(1)}, u32[]{:S(2)}, u32[]{:S(2)}) async-start(bf16[8,64,1024]{2,1,0:T(8,128)(2,1)} %bitcast.56), calls=%async_computation.5 | async-start | bytes 2097152 | tf_op jit(solution)/shard_map/all_to_all | solution.py:200
  165.1 1.2 convert_bitcast_fusion.1
  166.3 0.1 copy.19
  166.4 1.5 copy.21
  167.9 0.1 bitcast_select_fusion.1
  168.0 6.1 %chol_steps.3 = f32[512,512]{1,0:T(8,128)} custom-call(f32[512,512]{1,0:T(8,128)} %chol_steps.2.s_ref), custom_call_target="tpu_custom_call" | custom-call | flops 6000000000 | bytes 2000000 | tf_op jit(solution)/shard_map/chol_steps/pallas_call | solution.py:83
  174.1 3.2 %fusion.6 = f32[512,512]{1,0:T(8,128)S(1)} fusion(f32[512,512]{1,0:T(8,128)S(1)} %bitcast_select_fusion.1, f32[512,512]{1,0:T(8,128)} %chol_steps.3), kind=kOutput, calls=%fused_computation.33 | convolution fusion | flops 1610612736 | bytes 3145728 | tf_op jit(solution)/shard_map/dot_general | solution.py:280
  177.4 0.0 copy-done.1
  177.4 0.0 copy-start.3
  177.4 0.0 copy-start.4
  177.4 0.2 bitcast_select_fusion
  177.7 1.3 copy-done.4
  179.0 3.5 %convolution_convert_fusion = bf16[1024,512]{1,0:T(8,128)(2,1)S(1)} fusion(f32[1024,512]{1,0:T(8,128)S(1)} %bitcast_select_fusion, f32[512,512]{1,0:T(8,128)S(1)} %copy-done.4), kind=kOutput, calls=%fused_computation.7 | convolution fusion | flops 3221749760 | bytes 4194304 | tf_op jit(solution)/shard_map/dot_general | solution.py:281
  182.5 0.0 all-to-all-done.5
  182.5 0.2 copy.20
  182.7 0.0 copy-done.3
  182.7 1.8 fusion.2
  (11 shorter events, 0.1 us)
Async XLA Ops:
  0.6 13.2 %copy-start = (s32[8,24]{1,0:T(8,128)S(1)}, s32[8,24]{1,0:T(8,128)}, u32[]{:S(2)}) copy-start(s32[8,24]{1,0:T(8,128)} %param.5) | copy-start | bytes 2308
  2.4 21.3 %all-to-all-start = ((bf16[8,48,384]{2,1,0:T(8,128)(2,1)}), bf16[8,48,384]{2,1,0:T(8,128)(2,1)S(1)}, u32[]{:S(2)}, u32[]{:S(2)}) async-start(bf16[8,48,384]{2,1,0:T(8,128)(2,1)} %bitcast.5), calls=%async_computation | async-start | bytes 589824 | tf_op jit(solution)/shard_map/all_to_all | solution.py:200
  23.7 0.7 copy-start.6
  42.9 38.8 %all-to-all-start.1 = ((bf16[8,48,1024]{2,1,0:T(8,128)(2,1)}), bf16[8,48,1024]{2,1,0:T(8,128)(2,1)}, u32[]{:S(2)}, u32[]{:S(2)}) async-start(bf16[8,48,1024]{2,1,0:T(8,128)(2,1)} %expand_cols.1), calls=%async_computation.1 | async-start | bytes 1572864 | tf_op jit(solution)/shard_map/all_to_all | solution.py:200
  53.1 32.1 %copy-start.2 = (bf16[1024,512]{1,0:T(8,128)(2,1)S(1)}, bf16[1024,512]{1,0:T(8,128)(2,1)}, u32[]{:S(2)}) copy-start(bf16[1024,512]{1,0:T(8,128)(2,1)} %expand_pivot.1) | copy-start | bytes 3145732
  53.1 35.0 %copy-start.8 = (s32[4]{0:T(128)S(1)}, s32[4]{0:T(128)}, u32[]{:S(2)}) copy-start(s32[4]{0:T(128)} %param.7) | copy-start | bytes 52
  54.1 6.9 %collective-permute-start = (bf16[128,512]{1,0:T(8,128)(2,1)S(1)}, bf16[128,512]{1,0:T(8,128)(2,1)S(1)}, u32[]{:S(2)}, u32[]{:S(2)}) collective-permute-start(bf16[128,512]{1,0:T(8,128)(2,1)S(1)} %pad_maximum_fusion), channel_id=1, source_target_pairs={{0,64},{64,0},{128,192},{192,128},{256,320},{320,256},{384,448},{4... | collective-permute-start | bytes 393224 | tf_op jit(solution)/shard_map/ppermute | solution.py:186
  81.7 31.3 %all-to-all-start.3 = ((bf16[8,48,1024]{2,1,0:T(8,128)(2,1)}), bf16[8,48,1024]{2,1,0:T(8,128)(2,1)S(1)}, u32[]{:S(2)}, u32[]{:S(2)}) async-start(bf16[8,48,1024]{2,1,0:T(8,128)(2,1)} %all-to-all-done.1), calls=%async_computation.3 | async-start | bytes 1572864 | tf_op jit(solution)/shard_map/all_to_all | solution.py:200
  85.2 26.4 %collective-permute-start.2 = (bf16[1024,512]{1,0:T(8,128)(2,1)S(1)}, bf16[1024,512]{1,0:T(8,128)(2,1)S(1)}, u32[]{:S(2)}, u32[]{:S(2)}) collective-permute-start(bf16[1024,512]{1,0:T(8,128)(2,1)S(1)} %copy-done.2), channel_id=1, source_target_pairs={{0,64},{64,0},{128,192},{192,128},{256,320},{320,256},{384,448},{4... | collective-permute-start | bytes 3145736 | tf_op jit(solution)/shard_map/ppermute | solution.py:186
  113.0 5.3 %copy-start.5 = (bf16[8,48,1024]{2,1,0:T(8,128)(2,1)}, bf16[8,48,1024]{2,1,0:T(8,128)(2,1)S(1)}, u32[]{:S(2)}) copy-start(bf16[8,48,1024]{2,1,0:T(8,128)(2,1)S(1)} %all-to-all-done.3.x_ref) | copy-start | bytes 2359300
  113.0 45.3 %all-to-all-start.4 = ((bf16[8,128,512]{2,1,0:T(8,128)(2,1)}), bf16[8,128,512]{2,1,0:T(8,128)(2,1)S(1)}, u32[]{:S(2)}, u32[]{:S(2)}) async-start(bf16[8,128,512]{2,1,0:T(8,128)(2,1)} %bitcast.13), calls=%async_computation.4 | async-start | bytes 2097152 | tf_op jit(solution)/shard_map/all_to_all | solution.py:200
  121.5 36.8 %copy-start.7 = (bf16[512,1024]{1,0:T(8,128)(2,1)S(1)}, bf16[512,1024]{1,0:T(8,128)(2,1)}, u32[]{:S(2)}) copy-start(bf16[512,1024]{1,0:T(8,128)(2,1)} %get-tuple-element.32) | copy-start | bytes 3145732
  121.5 36.8 %collective-permute-start.1 = (bf16[512,1024]{1,0:T(8,128)(2,1)}, bf16[512,1024]{1,0:T(8,128)(2,1)S(1)}, u32[]{:S(2)}, u32[]{:S(2)}) collective-permute-start(bf16[512,1024]{1,0:T(8,128)(2,1)} %get-tuple-element.26), channel_id=1, source_target_pairs={{0,64},{64,0},{128,192},{192,128},{256,320},{320,256},{384,448},{4... | collective-permute-start | bytes 3145736 | tf_op jit(solution)/shard_map/ppermute | solution.py:186
  160.0 22.4 %all-to-all-start.5 = ((bf16[8,64,1024]{2,1,0:T(8,128)(2,1)}), bf16[8,64,1024]{2,1,0:T(8,128)(2,1)S(1)}, u32[]{:S(2)}, u32[]{:S(2)}) async-start(bf16[8,64,1024]{2,1,0:T(8,128)(2,1)} %bitcast.56), calls=%async_computation.5 | async-start | bytes 2097152 | tf_op jit(solution)/shard_map/all_to_all | solution.py:200
  174.1 3.2 %copy-start.1 = (f32[8,8,16,512]{3,2,1,0:T(8,128)S(1)}, f32[8,8,16,512]{3,2,1,0:T(8,128)}, u32[]{:S(2)}) copy-start(f32[8,8,16,512]{3,2,1,0:T(8,128)} %copy.21) | copy-start | bytes 6291460
  177.4 5.3 %copy-start.3 = (f32[512,512]{1,0:T(8,128)}, f32[512,512]{1,0:T(8,128)S(1)}, u32[]{:S(2)}) copy-start(f32[512,512]{1,0:T(8,128)S(1)} %fusion.6) | copy-start | bytes 3145732
  177.4 1.6 copy-start.4
